TPU v7x, 32 devices: a whole 2x2x4 slice. The times are simulated.
32 devices in a mesh: dp: 8 (over y, x, core), fsdp: 4 (over z).
Axes of the slice: x: 2, y: 2, z: 4, core: 2. Of those that a mesh axis runs over, the one named last changes fastest.
Arguments:
- tokens: bfloat16 [32768, 640], P(('dp', 'fsdp')), may hold values from -6 to 6
- cotangent: bfloat16 [32768, 640], P(('dp', 'fsdp')), may hold values from -6 to 6
- lengths: int32 [32, 4], P(('dp', 'fsdp')), may hold values from 1 to 768, 1024 in all within a row
- counts: int32 [32, 4], P(('dp', 'fsdp')), may hold values from 1 to 4
- w_qkv: float32 [1920, 640], P('fsdp', 'dp'), may hold values from -0.25 to 0.25
- w_out: float32 [640, 640], P('fsdp', 'dp'), may hold values from -2 to 2
- w_up: float32 [2560, 640], P('fsdp', 'dp'), may hold values from -0.25 to 0.25
- w_down: float32 [2560, 640], P('fsdp', 'dp'), may hold values from -0.125 to 0.125
- mom_qkv: float32 [1920, 640], P('fsdp', 'dp'), as said below
- mom_out: float32 [640, 640], P('fsdp', 'dp'), as said below
- mom_up: float32 [2560, 640], P('fsdp', 'dp'), as said below
- mom_down: float32 [2560, 640], P('fsdp', 'dp'), as said below
- vectors: float32 [13, 640], P(None, 'dp'), as said below
- vec_first: float32 [13, 640], P(None, 'dp'), as said below
- vec_second: float32 [13, 640], P(None, 'dp'), as said below
Outputs:
- layer_out: bfloat16 [32768, 640], P(('dp', 'fsdp'))
- input_grad: float32 [32768, 640], P(('dp', 'fsdp'))
- new_mom_qkv: float32 [1920, 640], P('fsdp', 'dp')
- new_mom_out: float32 [640, 640], P('fsdp', 'dp')
- new_mom_up: float32 [2560, 640], P('fsdp', 'dp')
- new_mom_down: float32 [2560, 640], P('fsdp', 'dp')
- new_w_qkv: float32 [1920, 640], P('fsdp', 'dp')
- new_w_out: float32 [640, 640], P('fsdp', 'dp')
- new_w_up: float32 [2560, 640], P('fsdp', 'dp')
- new_w_down: float32 [2560, 640], P('fsdp', 'dp')
- new_vectors: float32 [13, 640], P(None, 'dp')
- new_first: float32 [13, 640], P(None, 'dp')
- new_second: float32 [13, 640], P(None, 'dp')
Inputs may be any that keep to these rules, and one draw needn't show every extreme that they name: Each row's 4 lengths sum to 1024; the longest is exactly 768. `mom_qkv`: entries of both signs, about as large as the gradient of the same matrix. `mom_out`: entries of both signs, about as large as the gradient of the same matrix. `mom_up`: entries of both signs, about as large as the gradient of the same matrix. `mom_down`: entries of both signs, about as large as the gradient of the same matrix. `vectors`: gains between 0.7 and 1.3, shifts and biases of both signs. `vec_first`: entries of both signs. `vec_second`: positive entries.
All inputs are finite; a program needn't handle non-finite values.
Results may differ from a plain program's by a relative error of at most 0.0095.
The roundings to bfloat16 on the way count: a program that leaves them out, or rounds other values in their place, can miss the bound.
Values may be sent and summed in bfloat16 or wider, within the bound.
A program may use at most 192 MiB of HBM per device.

v0:
```python
import math

import jax
import jax.numpy as jnp
from jax import lax
from jax.sharding import PartitionSpec as P

HEAD_DIM = 32
NS_ITERS = 5
STEP = 10


norm_eps = 1e-05
masked_score = -1e30
poly_linear = 3.4445
poly_square = -4.775
poly_cubic = 2.0315
muon_rate = 0.5
muon_decay = 0.01
moment_keep = 0.5
adam_rate = 0.05
beta_first = 0.9
beta_second = 0.999
adam_eps = 1e-08


def layer_norm(values, gain_row, shift_row):
    center = values - jnp.mean(values, axis=-1, keepdims=True)
    spread = jnp.mean(center * center, axis=-1, keepdims=True)
    return center * lax.rsqrt(spread + norm_eps) * gain_row + shift_row


def gelu_exact(values):
    return 0.5 * values * (1.0 + lax.erf(values * (1.0 / math.sqrt(2.0))))


def rotate(values, cosine_table, sine_table):
    half_width = values.shape[-1] // 2
    turned = jnp.concatenate([-values[..., half_width:], values[..., :half_width]], axis=-1)
    return values * cosine_table + turned * sine_table


def rotary_tables(position, head_dim):
    indices = lax.broadcasted_iota(jnp.float32, (head_dim // 2,), 0)
    inverse = jnp.exp(indices * (-2.0 * math.log(10000.0) / head_dim))
    angles = position[..., None] * inverse
    angles = jnp.concatenate([angles, angles], axis=-1)
    return (jnp.cos(angles), jnp.sin(angles))


def row_layout(lengths, counts, row_len):
    row_count, slot_count = lengths.shape
    endings = jnp.cumsum(lengths, axis=1)
    starting = endings - lengths
    places = lax.broadcasted_iota(jnp.int32, (row_count, row_len), 1)
    segment = jnp.sum((places[:, :, None] >= endings[:, None, :]).astype(jnp.int32), axis=2)
    member = segment[:, :, None] == lax.broadcasted_iota(jnp.int32, (1, 1, slot_count), 2)
    first_place = jnp.sum(jnp.where(member, starting[:, None, :], 0), axis=2)
    position = (places - first_place).astype(jnp.float32)
    inverse_count = 1.0 / counts.astype(jnp.float32)
    seq_share = jnp.sum(jnp.where(member, inverse_count[:, None, :], 0.0), axis=2)
    return (segment, position, seq_share)


def rows_times_t(left_side, right_side):
    return lax.dot_general(
        left_side, right_side, (((1,), (1,)), ((), ())), preferred_element_type=jnp.float32
    )


def column_products(left_side, right_side):
    return lax.dot_general(
        left_side, right_side, (((0,), (0,)), ((), ())), preferred_element_type=jnp.float32
    )


def plain_product(left_side, right_side):
    return jnp.dot(left_side, right_side, preferred_element_type=jnp.float32)


def exact_product(left_side, right_side):
    return jnp.dot(left_side, right_side, precision=lax.Precision.HIGHEST)


def exact_gram(row_block):
    return lax.dot_general(
        row_block, row_block, (((0,), (0,)), ((), ())), precision=lax.Precision.HIGHEST
    )


def to_heads(values, row_count):
    return values.reshape(row_count, -1, values.shape[1], values.shape[2]).transpose(2, 0, 1, 3)


def from_heads(values):
    head_count, row_count, row_len, head_dim = values.shape
    return values.transpose(1, 2, 0, 3).reshape(row_count * row_len, head_count, head_dim)


def head_forward(same_segment):

    def attend_head(block_inputs):
        queries, key_rows, value_rows = block_inputs
        scores = jnp.einsum("rqd,rkd->rqk", queries, key_rows, preferred_element_type=jnp.float32)
        scores = jnp.where(same_segment, scores, masked_score)
        row_peak = jnp.max(scores, axis=-1, keepdims=True)
        raised = jnp.exp(scores - row_peak)
        row_total = jnp.sum(raised, axis=-1, keepdims=True)
        softmax_low = (raised / row_total).astype(jnp.bfloat16)
        attended = jnp.einsum(
            "rqk,rkd->rqd", softmax_low, value_rows, preferred_element_type=jnp.float32
        )
        return (attended, (row_peak + jnp.log(row_total))[..., 0])

    return attend_head


def head_backward(same_segment):

    def attend_back(block_inputs):
        queries, key_rows, value_rows, attn_grads, log_total = block_inputs
        scores = jnp.einsum("rqd,rkd->rqk", queries, key_rows, preferred_element_type=jnp.float32)
        scores = jnp.where(same_segment, scores, masked_score)
        softmax_full = jnp.exp(scores - log_total[..., None])
        weight_grad = jnp.einsum(
            "rqd,rkd->rqk", attn_grads, value_rows, preferred_element_type=jnp.float32
        )
        value_grad = jnp.einsum(
            "rqk,rqd->rkd",
            softmax_full.astype(jnp.bfloat16),
            attn_grads,
            preferred_element_type=jnp.float32,
        )
        row_center = jnp.sum(weight_grad * softmax_full, axis=-1, keepdims=True)
        score_grad = (softmax_full * (weight_grad - row_center)).astype(jnp.bfloat16)
        query_grad = jnp.einsum(
            "rqk,rkd->rqd", score_grad, key_rows, preferred_element_type=jnp.float32
        )
        key_grad = jnp.einsum(
            "rqk,rqd->rkd", score_grad, queries, preferred_element_type=jnp.float32
        )
        return (query_grad, key_grad, value_grad)

    return attend_back


def forward_pass(tokens, weights, same_segment, cosine_table, sine_table):
    w_qkv, w_out, w_up, w_down, vectors = weights
    table = vectors.astype(jnp.float32)
    row_count = same_segment.shape[0]
    width = tokens.shape[1]
    head_count = width // HEAD_DIM
    inputs = tokens.astype(jnp.float32)
    normed_one = layer_norm(inputs, table[0], table[1]).astype(jnp.bfloat16)
    project = rows_times_t(normed_one, w_qkv) + table[4:7].reshape(-1)
    query_scale = 1.0 / math.sqrt(HEAD_DIM)
    queries = project[:, :width].reshape(-1, head_count, HEAD_DIM) * query_scale
    key_rows = project[:, width : 2 * width].reshape(-1, head_count, HEAD_DIM)
    value_rows = project[:, 2 * width :].reshape(-1, head_count, HEAD_DIM).astype(jnp.bfloat16)
    head_q = to_heads(rotate(queries, cosine_table, sine_table).astype(jnp.bfloat16), row_count)
    head_k = to_heads(rotate(key_rows, cosine_table, sine_table).astype(jnp.bfloat16), row_count)
    head_v = to_heads(value_rows, row_count)
    attended, log_total = lax.map(head_forward(same_segment), (head_q, head_k, head_v))
    attn_low = from_heads(attended).reshape(-1, width).astype(jnp.bfloat16)
    after_attn = inputs + (rows_times_t(attn_low, w_out) + table[7])
    normed_two = layer_norm(after_attn, table[2], table[3]).astype(jnp.bfloat16)
    hidden_pre = rows_times_t(normed_two, w_up) + table[9:].reshape(-1)
    hidden_low = gelu_exact(hidden_pre).astype(jnp.bfloat16)
    result = after_attn + (plain_product(hidden_low, w_down) + table[8])
    kept_values = (
        inputs,
        normed_one,
        head_q,
        head_k,
        head_v,
        log_total,
        attn_low,
        after_attn,
        normed_two,
        hidden_pre,
        hidden_low,
    )
    return (result.astype(jnp.bfloat16), kept_values)


def backward_pass(
    cotangent, seq_share, weights, kept_values, same_segment, cosine_table, sine_table
):
    w_qkv, w_out, w_up, w_down, vectors = weights
    table = vectors.astype(jnp.float32)
    (
        inputs,
        normed_one,
        head_q,
        head_k,
        head_v,
        log_total,
        attn_low,
        after_attn,
        normed_two,
        hidden_pre,
        hidden_low,
    ) = kept_values
    row_count = same_segment.shape[0]
    width = inputs.shape[1]
    head_count = width // HEAD_DIM
    incoming = cotangent.astype(jnp.float32) * seq_share.reshape(-1)[:, None]
    grad_low = incoming.astype(jnp.bfloat16)
    grad_down = column_products(hidden_low, grad_low)
    bias_down_grad = jnp.sum(grad_low.astype(jnp.float32), axis=0)
    hidden_grad = rows_times_t(grad_low, w_down)
    gelu_value, gelu_pull = jax.vjp(gelu_exact, hidden_pre)
    pre_grad = gelu_pull(hidden_grad)[0].astype(jnp.bfloat16)
    grad_up = column_products(pre_grad, normed_two)
    bias_up_grad = jnp.sum(pre_grad.astype(jnp.float32), axis=0)
    normed_two_grad = plain_product(pre_grad, w_up)
    norm_two_value, norm_two_pull = jax.vjp(layer_norm, after_attn, table[2], table[3])
    resid_grad, gain_two_grad, shift_two_grad = norm_two_pull(normed_two_grad)
    after_grad = incoming + resid_grad
    branch_low = after_grad.astype(jnp.bfloat16)
    grad_out = column_products(branch_low, attn_low)
    bias_out_grad = jnp.sum(branch_low.astype(jnp.float32), axis=0)
    attn_grad = plain_product(branch_low, w_out).astype(jnp.bfloat16)
    head_grad = to_heads(attn_grad.reshape(-1, head_count, HEAD_DIM), row_count)
    query_grad, key_grad, value_grad = lax.map(
        head_backward(same_segment), (head_q, head_k, head_v, head_grad, log_total)
    )
    query_rows = from_heads(query_grad)
    turn_value, turn_pull = jax.vjp(
        lambda values: rotate(values, cosine_table, sine_table), query_rows
    )
    query_back = turn_pull(query_rows)[0] * (1.0 / math.sqrt(HEAD_DIM))
    key_back = turn_pull(from_heads(key_grad))[0]
    proj_grad = jnp.concatenate(
        [
            query_back.reshape(-1, width),
            key_back.reshape(-1, width),
            from_heads(value_grad).reshape(-1, width),
        ],
        axis=1,
    ).astype(jnp.bfloat16)
    grad_qkv = column_products(proj_grad, normed_one)
    bias_qkv_grad = jnp.sum(proj_grad.astype(jnp.float32), axis=0)
    normed_one_grad = plain_product(proj_grad, w_qkv)
    norm_one_value, norm_one_pull = jax.vjp(layer_norm, inputs, table[0], table[1])
    in_grad, gain_one_grad, shift_one_grad = norm_one_pull(normed_one_grad)
    input_grad = after_grad + in_grad
    vector_grad = jnp.concatenate(
        [
            gain_one_grad[None],
            shift_one_grad[None],
            gain_two_grad[None],
            shift_two_grad[None],
            bias_qkv_grad.reshape(3, width),
            bias_out_grad[None],
            bias_down_grad[None],
            bias_up_grad.reshape(-1, width),
        ],
        axis=0,
    )
    return (input_grad, (grad_qkv, grad_out, grad_up, grad_down, vector_grad))


def polynomial(gram_now, identity):
    return (
        poly_linear * identity
        + poly_square * gram_now
        + poly_cubic * exact_product(gram_now, gram_now)
    )


def orthogonalize(row_blocks):
    identity = jnp.eye(row_blocks[0].shape[1], dtype=jnp.float32)
    current = row_blocks
    for iteration in range(NS_ITERS):
        gram_pieces = (
            lax.psum_scatter(exact_gram(current[0]), "fsdp", scatter_dimension=0, tiled=True),
            lax.psum_scatter(exact_gram(current[1]), "fsdp", scatter_dimension=0, tiled=True),
            lax.psum_scatter(exact_gram(current[2]), "fsdp", scatter_dimension=0, tiled=True),
            lax.psum_scatter(exact_gram(current[3]), "fsdp", scatter_dimension=0, tiled=True),
        )
        gram_full = (
            lax.all_gather(gram_pieces[0], "fsdp", axis=0, tiled=True),
            lax.all_gather(gram_pieces[1], "fsdp", axis=0, tiled=True),
            lax.all_gather(gram_pieces[2], "fsdp", axis=0, tiled=True),
            lax.all_gather(gram_pieces[3], "fsdp", axis=0, tiled=True),
        )
        if iteration == 0:
            norm_sq = [jnp.trace(gram_now) + 1e-07 for gram_now in gram_full]
            current = tuple(
                (row_block * lax.rsqrt(scale_sq) for row_block, scale_sq in zip(current, norm_sq))
            )
            gram_full = tuple(
                (gram_now / scale_sq for gram_now, scale_sq in zip(gram_full, norm_sq))
            )
        current = tuple(
            (
                exact_product(row_block, polynomial(gram_now, identity))
                for row_block, gram_now in zip(current, gram_full)
            )
        )
    return current


def shards(
    tokens,
    cotangent,
    lengths,
    counts,
    w_qkv,
    w_out,
    w_up,
    w_down,
    mom_qkv,
    mom_out,
    mom_up,
    mom_down,
    vectors,
    vec_first,
    vec_second,
):
    row_len = tokens.shape[0] // lengths.shape[0]
    segment, position, seq_share = row_layout(lengths, counts, row_len)
    same_segment = segment[:, :, None] == segment[:, None, :]
    cosine_table, sine_table = rotary_tables(position.reshape(-1), HEAD_DIM)
    cosine_table = cosine_table[:, None, :]
    sine_table = sine_table[:, None, :]
    low_rows = (
        lax.all_gather(w_qkv.astype(jnp.bfloat16), "fsdp", axis=0, tiled=True),
        lax.all_gather(w_out.astype(jnp.bfloat16), "fsdp", axis=0, tiled=True),
        lax.all_gather(w_up.astype(jnp.bfloat16), "fsdp", axis=0, tiled=True),
        lax.all_gather(w_down.astype(jnp.bfloat16), "fsdp", axis=0, tiled=True),
    )
    weights = (
        lax.all_gather(low_rows[0], "dp", axis=1, tiled=True),
        lax.all_gather(low_rows[1], "dp", axis=1, tiled=True),
        lax.all_gather(low_rows[2], "dp", axis=1, tiled=True),
        lax.all_gather(low_rows[3], "dp", axis=1, tiled=True),
        lax.all_gather(vectors.astype(jnp.bfloat16), "dp", axis=1, tiled=True),
    )
    layer_out, kept_values = forward_pass(tokens, weights, same_segment, cosine_table, sine_table)
    again_rows = (
        lax.all_gather(w_qkv.astype(jnp.bfloat16), "fsdp", axis=0, tiled=True),
        lax.all_gather(w_out.astype(jnp.bfloat16), "fsdp", axis=0, tiled=True),
        lax.all_gather(w_up.astype(jnp.bfloat16), "fsdp", axis=0, tiled=True),
        lax.all_gather(w_down.astype(jnp.bfloat16), "fsdp", axis=0, tiled=True),
    )
    weights_back = (
        lax.all_gather(again_rows[0], "dp", axis=1, tiled=True),
        lax.all_gather(again_rows[1], "dp", axis=1, tiled=True),
        lax.all_gather(again_rows[2], "dp", axis=1, tiled=True),
        lax.all_gather(again_rows[3], "dp", axis=1, tiled=True),
        lax.all_gather(vectors.astype(jnp.bfloat16), "dp", axis=1, tiled=True),
    )
    repeated_out, values_back = forward_pass(
        tokens, weights_back, same_segment, cosine_table, sine_table
    )
    input_grad, grad_parts = backward_pass(
        cotangent, seq_share, weights_back, values_back, same_segment, cosine_table, sine_table
    )
    column_sums = (
        lax.psum_scatter(grad_parts[0], "dp", scatter_dimension=1, tiled=True),
        lax.psum_scatter(grad_parts[1], "dp", scatter_dimension=1, tiled=True),
        lax.psum_scatter(grad_parts[2], "dp", scatter_dimension=1, tiled=True),
        lax.psum_scatter(grad_parts[3], "dp", scatter_dimension=1, tiled=True),
        lax.psum_scatter(grad_parts[4], "dp", scatter_dimension=1, tiled=True),
    )
    matrix_grads = (
        lax.psum_scatter(column_sums[0], "fsdp", scatter_dimension=0, tiled=True),
        lax.psum_scatter(column_sums[1], "fsdp", scatter_dimension=0, tiled=True),
        lax.psum_scatter(column_sums[2], "fsdp", scatter_dimension=0, tiled=True),
        lax.psum_scatter(column_sums[3], "fsdp", scatter_dimension=0, tiled=True),
    )
    vector_grad = lax.psum(column_sums[4], "fsdp")
    old_weights = (w_qkv, w_out, w_up, w_down)
    old_moments = (mom_qkv, mom_out, mom_up, mom_down)
    new_moments = tuple(
        (
            moment_keep * moment_old + grad_now
            for moment_old, grad_now in zip(old_moments, matrix_grads)
        )
    )
    row_blocks = (
        lax.all_gather(new_moments[0], "dp", axis=1, tiled=True),
        lax.all_gather(new_moments[1], "dp", axis=1, tiled=True),
        lax.all_gather(new_moments[2], "dp", axis=1, tiled=True),
        lax.all_gather(new_moments[3], "dp", axis=1, tiled=True),
    )
    orthogonals = orthogonalize(row_blocks)
    columns = w_qkv.shape[1]
    col_start = lax.axis_index("dp") * columns
    fsdp_count = lax.axis_size("fsdp")
    new_weights = []
    for weight_old, orthogonal in zip(old_weights, orthogonals):
        rows_full = orthogonal.shape[0] * fsdp_count
        factor = muon_rate * math.sqrt(max(1.0, rows_full / orthogonal.shape[1]))
        own_cols = lax.dynamic_slice_in_dim(orthogonal, col_start, columns, 1)
        new_weights.append(weight_old * (1.0 - muon_rate * muon_decay) - factor * own_cols)
    new_first = beta_first * vec_first + (1.0 - beta_first) * vector_grad
    new_second = beta_second * vec_second + (1.0 - beta_second) * vector_grad * vector_grad
    first_fix = 1.0 - beta_first**STEP
    second_fix = 1.0 - beta_second**STEP
    new_vectors = vectors - adam_rate * (new_first / first_fix) / (
        jnp.sqrt(new_second / second_fix) + adam_eps
    )
    return (
        layer_out,
        input_grad,
        new_moments[0],
        new_moments[1],
        new_moments[2],
        new_moments[3],
        new_weights[0],
        new_weights[1],
        new_weights[2],
        new_weights[3],
        new_vectors,
        new_first,
        new_second,
    )


def solution(mesh):
    placed = (
        P(("dp", "fsdp"), None),
        P(("dp", "fsdp"), None),
        P(("dp", "fsdp"), None),
        P(("dp", "fsdp"), None),
        P("fsdp", "dp"),
        P("fsdp", "dp"),
        P("fsdp", "dp"),
        P("fsdp", "dp"),
        P("fsdp", "dp"),
        P("fsdp", "dp"),
        P("fsdp", "dp"),
        P("fsdp", "dp"),
        P(None, "dp"),
        P(None, "dp"),
        P(None, "dp"),
    )
    return jax.shard_map(
        shards,
        mesh=mesh,
        in_specs=placed,
        out_specs=(
            P(("dp", "fsdp"), None),
            P(("dp", "fsdp"), None),
            P("fsdp", "dp"),
            P("fsdp", "dp"),
            P("fsdp", "dp"),
            P("fsdp", "dp"),
            P("fsdp", "dp"),
            P("fsdp", "dp"),
            P("fsdp", "dp"),
            P("fsdp", "dp"),
            P(None, "dp"),
            P(None, "dp"),
            P(None, "dp"),
        ),
        check_vma=False,
    )
```

profile of v0, /device:TPU:0, one launch (start us, length us, event | category | flops | bytes accessed | tf_op | source)
XLA Modules:
  0.0 2671.5 jit_solution(3990797646878700355)
XLA Ops:
  125.8 97.4 %while.43 = (s32[]{:T(128)}, bf16[20,1,1024,32]{2,3,1,0:T(8,128)(2,1)S(1)}, f32[20,1,1024]{2,1,0:T(1,128)S(1)}, bf16[20,1,1024,32]{3,2,1,0:T(8,128)(2,1)}, bf16[...) while((s32[]{:T(128)}, ...), condition=%wide.region_15.16_spmd.clone.clone, body=%wide.region_12.15_spmd.clone.sunk.clone | while | flops 146799616 | bytes 13563993 | solution.py:163
  246.2 63.1 %reduce-scatter.44.cloned.1.call-done = f32[2560,80]{0,1:T(8,128)} async-done(((f32[2560,640]{0,1:T(8,128)}), f32[2560,80]{0,1:T(8,128)}) %reduce-scatter.44.cloned.1.call-update) | async-done | bytes 819216 | tf_op jit(solution)/shard_map/reduce_scatter | solution.py:365
  370.8 36.4 %reduce-scatter.78.cloned.1.call-done = f32[160,640]{1,0:T(8,128)} async-done(((f32[640,640]{1,0:T(8,128)}), f32[160,640]{1,0:T(8,128)}) %reduce-scatter.78.cloned.1.call-update) | async-done | bytes 409616 | tf_op jit(solution)/shard_map/reduce_scatter | solution.py:280
  407.5 38.5 %all-gather.71.cloned.1.call-done = f32[640,640]{1,0:T(8,128)} async-done(((f32[160,640]{1,0:T(8,128)}), f32[640,640]{1,0:T(8,128)}) %all-gather.71.cloned.1.call-update) | async-done | bytes 1638416 | tf_op jit(solution)/shard_map/all_gather | solution.py:286
  466.6 35.3 %reduce-scatter.80.cloned.1.call-done = f32[160,640]{1,0:T(8,128)} async-done(((f32[640,640]{1,0:T(8,128)}), f32[160,640]{1,0:T(8,128)}) %reduce-scatter.80.cloned.1.call-update) | async-done | bytes 409616 | tf_op jit(solution)/shard_map/reduce_scatter | solution.py:280
  502.0 38.8 %all-gather.73.cloned.1.call-done = f32[640,640]{1,0:T(8,128)} async-done(((f32[160,640]{1,0:T(8,128)}), f32[640,640]{1,0:T(8,128)}) %all-gather.73.cloned.1.call-update) | async-done | bytes 1638416 | tf_op jit(solution)/shard_map/all_gather | solution.py:286
  559.9 35.3 %reduce-scatter.82.cloned.1.call-done = f32[160,640]{1,0:T(8,128)} async-done(((f32[640,640]{1,0:T(8,128)}), f32[160,640]{1,0:T(8,128)}) %reduce-scatter.82.cloned.1.call-update) | async-done | bytes 409616 | tf_op jit(solution)/shard_map/reduce_scatter | solution.py:280
  595.2 38.7 %all-gather.75.cloned.1.call-done = f32[640,640]{1,0:T(8,128)} async-done(((f32[160,640]{1,0:T(8,128)}), f32[640,640]{1,0:T(8,128)}) %all-gather.75.cloned.1.call-update) | async-done | bytes 1638416 | tf_op jit(solution)/shard_map/all_gather | solution.py:286
  653.4 35.3 %reduce-scatter.84.cloned.1.call-done = f32[160,640]{1,0:T(8,128)} async-done(((f32[640,640]{1,0:T(8,128)}), f32[160,640]{1,0:T(8,128)}) %reduce-scatter.84.cloned.1.call-update) | async-done | bytes 409616 | tf_op jit(solution)/shard_map/reduce_scatter | solution.py:280
  688.8 38.8 %all-gather.77.cloned.1.call-done = f32[640,640]{1,0:T(8,128)} async-done(((f32[160,640]{1,0:T(8,128)}), f32[640,640]{1,0:T(8,128)}) %all-gather.77.cloned.1.call-update) | async-done | bytes 1638416 | tf_op jit(solution)/shard_map/all_gather | solution.py:286
  746.7 35.3 %reduce-scatter.86.cloned.1.call-done = f32[160,640]{1,0:T(8,128)} async-done(((f32[640,640]{1,0:T(8,128)}), f32[160,640]{1,0:T(8,128)}) %reduce-scatter.86.cloned.1.call-update) | async-done | bytes 409616 | tf_op jit(solution)/shard_map/reduce_scatter | solution.py:280
  782.0 38.6 %all-gather.79.cloned.1.call-done = f32[640,640]{1,0:T(8,128)} async-done(((f32[160,640]{1,0:T(8,128)}), f32[640,640]{1,0:T(8,128)}) %all-gather.79.cloned.1.call-update) | async-done | bytes 1638416 | tf_op jit(solution)/shard_map/all_gather | solution.py:286
  849.1 31.3 %all-gather.33.cloned.1.call-done = bf16[2560,640]{0,1:T(8,128)(2,1)} async-done(((bf16[2560,80]{0,1:T(8,128)(2,1)}), bf16[2560,640]{0,1:T(8,128)(2,1)}) %all-gather.33.cloned.1.call-update) | async-done | bytes 3276816 | tf_op jit(solution)/shard_map/all_gather | solution.py:338
  916.4 242.6 %while.44 = (s32[]{:T(128)}, f32[20,1,1024,32]{2,3,1,0:T(8,128)}, f32[20,1,1024,32]{2,3,1,0:T(8,128)}, bf16[20,1,1024,32]{2,3,1,0:T(8,128)(2,1)S(1)}, bf16[20,1,...) while((s32[]{:T(128)}, f32[20,1,1024,32]{2,3,1,0:T(8,128)}, ...), condition=%wide.region_22.23_spmd.clone.clone, body=%wide.region_20.22_spmd.clone.sunk.clone | while | flops 351271936 | bytes 33739888 | solution.py:225
  1189.3 39.6 %reduce-scatter.36.cloned.1.call-done = f32[1920,80]{0,1:T(8,128)} async-done(((f32[1920,640]{0,1:T(8,128)}), f32[1920,80]{0,1:T(8,128)}) %reduce-scatter.36.cloned.1.call-update) | async-done | bytes 614416 | tf_op jit(solution)/shard_map/reduce_scatter | solution.py:362
  1231.3 64.3 %reduce-scatter.40.cloned.1.call-done = f32[2560,80]{0,1:T(8,128)} async-done(((f32[2560,640]{0,1:T(8,128)}), f32[2560,80]{0,1:T(8,128)}) %reduce-scatter.40.cloned.1.call-update) | async-done | bytes 819216 | tf_op jit(solution)/shard_map/reduce_scatter | solution.py:364
  1295.7 42.7 %reduce-scatter.38.cloned.1.call-done = f32[640,80]{0,1:T(8,128)} async-done(((f32[640,640]{0,1:T(8,128)}), f32[640,80]{0,1:T(8,128)}) %reduce-scatter.38.cloned.1.call-update) | async-done | bytes 204816 | tf_op jit(solution)/shard_map/reduce_scatter | solution.py:363
  1475.4 30.9 %reduce-scatter.58.cloned.1.call-done = f32[160,640]{1,0:T(8,128)} async-done(((f32[640,640]{1,0:T(8,128)}), f32[160,640]{1,0:T(8,128)}) %reduce-scatter.58.cloned.1.call-update) | async-done | bytes 409616 | tf_op jit(solution)/shard_map/reduce_scatter | solution.py:278
  1506.4 38.0 %reduce-scatter.48.cloned.1.call-done = f32[160,640]{1,0:T(8,128)} async-done(((f32[640,640]{1,0:T(8,128)}), f32[160,640]{1,0:T(8,128)}) %reduce-scatter.48.cloned.1.call-update) | async-done | bytes 409616 | tf_op jit(solution)/shard_map/reduce_scatter | solution.py:277
  1544.5 37.5 %reduce-scatter.68.cloned.1.call-done = f32[160,640]{1,0:T(8,128)} async-done(((f32[640,640]{1,0:T(8,128)}), f32[160,640]{1,0:T(8,128)}) %reduce-scatter.68.cloned.1.call-update) | async-done | bytes 409616 | tf_op jit(solution)/shard_map/reduce_scatter | solution.py:279
  1582.3 38.5 %all-gather.47.cloned.1.call-done = f32[640,640]{1,0:T(8,128)} async-done(((f32[160,640]{1,0:T(8,128)}), f32[640,640]{1,0:T(8,128)}) %all-gather.47.cloned.1.call-update) | async-done | bytes 1638416 | tf_op jit(solution)/shard_map/all_gather | solution.py:284
  1735.5 38.3 %reduce-scatter.50.cloned.1.call-done = f32[160,640]{1,0:T(8,128)} async-done(((f32[640,640]{1,0:T(8,128)}), f32[160,640]{1,0:T(8,128)}) %reduce-scatter.50.cloned.1.call-update) | async-done | bytes 409616 | tf_op jit(solution)/shard_map/reduce_scatter | solution.py:277
  1773.9 37.4 %reduce-scatter.70.cloned.1.call-done = f32[160,640]{1,0:T(8,128)} async-done(((f32[640,640]{1,0:T(8,128)}), f32[160,640]{1,0:T(8,128)}) %reduce-scatter.70.cloned.1.call-update) | async-done | bytes 409616 | tf_op jit(solution)/shard_map/reduce_scatter | solution.py:279
  1811.4 38.8 %all-gather.49.cloned.1.call-done = f32[640,640]{1,0:T(8,128)} async-done(((f32[160,640]{1,0:T(8,128)}), f32[640,640]{1,0:T(8,128)}) %all-gather.49.cloned.1.call-update) | async-done | bytes 1638416 | tf_op jit(solution)/shard_map/all_gather | solution.py:284
  1965.0 38.2 %reduce-scatter.52.cloned.1.call-done = f32[160,640]{1,0:T(8,128)} async-done(((f32[640,640]{1,0:T(8,128)}), f32[160,640]{1,0:T(8,128)}) %reduce-scatter.52.cloned.1.call-update) | async-done | bytes 409616 | tf_op jit(solution)/shard_map/reduce_scatter | solution.py:277
  2003.2 37.6 %reduce-scatter.72.cloned.1.call-done = f32[160,640]{1,0:T(8,128)} async-done(((f32[640,640]{1,0:T(8,128)}), f32[160,640]{1,0:T(8,128)}) %reduce-scatter.72.cloned.1.call-update) | async-done | bytes 409616 | tf_op jit(solution)/shard_map/reduce_scatter | solution.py:279
  2040.8 38.7 %all-gather.51.cloned.1.call-done = f32[640,640]{1,0:T(8,128)} async-done(((f32[160,640]{1,0:T(8,128)}), f32[640,640]{1,0:T(8,128)}) %all-gather.51.cloned.1.call-update) | async-done | bytes 1638416 | tf_op jit(solution)/shard_map/all_gather | solution.py:284
  2194.2 38.3 %reduce-scatter.54.cloned.1.call-done = f32[160,640]{1,0:T(8,128)} async-done(((f32[640,640]{1,0:T(8,128)}), f32[160,640]{1,0:T(8,128)}) %reduce-scatter.54.cloned.1.call-update) | async-done | bytes 409616 | tf_op jit(solution)/shard_map/reduce_scatter | solution.py:277
  2232.6 37.5 %reduce-scatter.74.cloned.1.call-done = f32[160,640]{1,0:T(8,128)} async-done(((f32[640,640]{1,0:T(8,128)}), f32[160,640]{1,0:T(8,128)}) %reduce-scatter.74.cloned.1.call-update) | async-done | bytes 409616 | tf_op jit(solution)/shard_map/reduce_scatter | solution.py:279
  2270.1 38.6 %all-gather.53.cloned.1.call-done = f32[640,640]{1,0:T(8,128)} async-done(((f32[160,640]{1,0:T(8,128)}), f32[640,640]{1,0:T(8,128)}) %all-gather.53.cloned.1.call-update) | async-done | bytes 1638416 | tf_op jit(solution)/shard_map/all_gather | solution.py:284
  2424.7 125.5 %while.42 = (s32[]{:T(128)}, bf16[20,1,1024,32]{2,3,1,0:T(8,128)(2,1)}, bf16[20,1,1024,32]{3,2,1,0:T(8,128)(2,1)}, bf16[20,1,1024,32]{3,2,1,0:T(8,128)(2,1)}, bf...) while((s32[]{:T(128)}, bf16[20,1,1024,32]{2,3,1,0:T(8,128)(2,1)}, ...), condition=%wide.region_8.9_spmd.clone.clone, body=%wide.region_5.8_spmd.clone.sunk.clone | while | flops 146798592 | bytes 24029316 | solution.py:163
  2624.3 27.5 %all-gather.67.cloned.1.call-done = f32[640,640]{1,0:T(8,128)} async-done(((f32[160,640]{1,0:T(8,128)}), f32[640,640]{1,0:T(8,128)}) %all-gather.67.cloned.1.call-update) | async-done | bytes 1638416 | tf_op jit(solution)/shard_map/all_gather | solution.py:285
  (906 shorter events, 1521.1 us)
Async XLA Ops:
  25.4 202.8 %all-gather.31.cloned.1.call-start = ((), (), s32[]{:S(2)}) async-start(), calls=%async_computation.30 | async-start | bytes 3686400 | tf_op jit(solution)/shard_map/all_gather | solution.py:337
  41.8 267.5 %reduce-scatter.44.cloned.1.call-start = ((), (), s32[]{:S(2)}) async-start(), calls=%async_computation.36 | async-start | bytes 7372800 | tf_op jit(solution)/shard_map/reduce_scatter | solution.py:365
  848.8 380.1 %reduce-scatter.36.cloned.1.call-start = ((), (), s32[]{:S(2)}) async-start(), calls=%async_computation.32 | async-start | bytes 5529600 | tf_op jit(solution)/shard_map/reduce_scatter | solution.py:362
  1183.9 154.4 %reduce-scatter.38.cloned.1.call-start = ((), (), s32[]{:S(2)}) async-start(), calls=%async_computation.33 | async-start | bytes 1843200 | tf_op jit(solution)/shard_map/reduce_scatter | solution.py:363
  1189.2 177.4 %reduce-scatter.88.cloned.1.call-start = ((), (), s32[]{:S(2)}) async-start(), calls=%async_computation.81 | async-start | bytes 1228800
  1231.3 160.0 %reduce-scatter.42.cloned.1.call-start = ((), (), s32[]{:S(2)}) async-start(), calls=%async_computation.35 | async-start | bytes 1024000 | tf_op jit(solution)/shard_map/reduce_scatter | solution.py:371
  1445.4 136.7 %reduce-scatter.68.cloned.1.call-start = ((), (), s32[]{:S(2)}) async-start(), calls=%async_computation.60 | async-start | bytes 2048000 | tf_op jit(solution)/shard_map/reduce_scatter | solution.py:279
  1475.4 145.5 %all-gather.47.cloned.1.call-start = ((), (), s32[]{:S(2)}) async-start(), calls=%async_computation.50 | async-start | bytes 2048000 | tf_op jit(solution)/shard_map/all_gather | solution.py:284
  1506.4 153.1 %all-gather.37.cloned.1.call-start = ((), (), s32[]{:S(2)}) async-start(), calls=%async_computation.40 | async-start | bytes 2048000 | tf_op jit(solution)/shard_map/all_gather | solution.py:283
  1544.5 153.5 %all-gather.59.cloned.1.call-start = ((), (), s32[]{:S(2)}) async-start(), calls=%async_computation.61 | async-start | bytes 2048000 | tf_op jit(solution)/shard_map/all_gather | solution.py:285
  1582.1 153.4 %reduce-scatter.60.cloned.1.call-start = ((), (), s32[]{:S(2)}) async-start(), calls=%async_computation.51 | async-start | bytes 2048000 | tf_op jit(solution)/shard_map/reduce_scatter | solution.py:278
  1635.1 138.7 %reduce-scatter.50.cloned.1.call-start = ((), (), s32[]{:S(2)}) async-start(), calls=%async_computation.41 | async-start | bytes 2048000 | tf_op jit(solution)/shard_map/reduce_scatter | solution.py:277
  1677.6 133.7 %reduce-scatter.70.cloned.1.call-start = ((), (), s32[]{:S(2)}) async-start(), calls=%async_computation.62 | async-start | bytes 2048000 | tf_op jit(solution)/shard_map/reduce_scatter | solution.py:279
  1735.5 153.4 %all-gather.39.cloned.1.call-start = ((), (), s32[]{:S(2)}) async-start(), calls=%async_computation.42 | async-start | bytes 2048000 | tf_op jit(solution)/shard_map/all_gather | solution.py:283
  1773.8 153.6 %all-gather.61.cloned.1.call-start = ((), (), s32[]{:S(2)}) async-start(), calls=%async_computation.63 | async-start | bytes 2048000 | tf_op jit(solution)/shard_map/all_gather | solution.py:285
  1811.3 153.6 %reduce-scatter.62.cloned.1.call-start = ((), (), s32[]{:S(2)}) async-start(), calls=%async_computation.53 | async-start | bytes 2048000 | tf_op jit(solution)/shard_map/reduce_scatter | solution.py:278
  1861.6 141.6 %reduce-scatter.52.cloned.1.call-start = ((), (), s32[]{:S(2)}) async-start(), calls=%async_computation.43 | async-start | bytes 2048000 | tf_op jit(solution)/shard_map/reduce_scatter | solution.py:277
  1905.3 135.5 %reduce-scatter.72.cloned.1.call-start = ((), (), s32[]{:S(2)}) async-start(), calls=%async_computation.64 | async-start | bytes 2048000 | tf_op jit(solution)/shard_map/reduce_scatter | solution.py:279
  1946.6 132.9 %all-gather.51.cloned.1.call-start = ((), (), s32[]{:S(2)}) async-start(), calls=%async_computation.54 | async-start | bytes 2048000 | tf_op jit(solution)/shard_map/all_gather | solution.py:284
  1964.9 153.3 %all-gather.41.cloned.1.call-start = ((), (), s32[]{:S(2)}) async-start(), calls=%async_computation.44 | async-start | bytes 2048000 | tf_op jit(solution)/shard_map/all_gather | solution.py:283
  2003.2 153.7 %all-gather.63.cloned.1.call-start = ((), (), s32[]{:S(2)}) async-start(), calls=%async_computation.65 | async-start | bytes 2048000 | tf_op jit(solution)/shard_map/all_gather | solution.py:285
  2040.8 153.4 %reduce-scatter.64.cloned.1.call-start = ((), (), s32[]{:S(2)}) async-start(), calls=%async_computation.55 | async-start | bytes 2048000 | tf_op jit(solution)/shard_map/reduce_scatter | solution.py:278
  2091.7 140.8 %reduce-scatter.54.cloned.1.call-start = ((), (), s32[]{:S(2)}) async-start(), calls=%async_computation.45 | async-start | bytes 2048000 | tf_op jit(solution)/shard_map/reduce_scatter | solution.py:277
  2134.5 135.5 %reduce-scatter.74.cloned.1.call-start = ((), (), s32[]{:S(2)}) async-start(), calls=%async_computation.66 | async-start | bytes 2048000 | tf_op jit(solution)/shard_map/reduce_scatter | solution.py:279
  2194.2 153.1 %all-gather.43.cloned.1.call-start = ((), (), s32[]{:S(2)}) async-start(), calls=%async_computation.46 | async-start | bytes 2048000 | tf_op jit(solution)/shard_map/all_gather | solution.py:283
  2232.5 153.3 %all-gather.65.cloned.1.call-start = ((), (), s32[]{:S(2)}) async-start(), calls=%async_computation.67 | async-start | bytes 2048000 | tf_op jit(solution)/shard_map/all_gather | solution.py:285
  2270.0 154.1 %reduce-scatter.66.cloned.1.call-start = ((), (), s32[]{:S(2)}) async-start(), calls=%async_computation.57 | async-start | bytes 2048000 | tf_op jit(solution)/shard_map/reduce_scatter | solution.py:278
  2320.2 234.8 %reduce-scatter.56.cloned.1.call-start = ((), (), s32[]{:S(2)}) async-start(), calls=%async_computation.47 | async-start | bytes 2048000 | tf_op jit(solution)/shard_map/reduce_scatter | solution.py:277
  2363.6 208.8 %reduce-scatter.76.cloned.1.call-start = ((), (), s32[]{:S(2)}) async-start(), calls=%async_computation.68 | async-start | bytes 2048000 | tf_op jit(solution)/shard_map/reduce_scatter | solution.py:279
  2405.1 176.2 %reduce-scatter.92.cloned.1.call-start = ((), (), s32[]{:S(2)}) async-start(), calls=%async_computation.83 | async-start | bytes 368640
  2424.1 169.1 %all-gather.55.cloned.1.call-start = ((), (), s32[]{:S(2)}) async-start(), calls=%async_computation.58 | async-start | bytes 2048000 | tf_op jit(solution)/shard_map/all_gather | solution.py:284
  2424.7 188.5 %all-gather.45.cloned.1.call-start = ((), (), s32[]{:S(2)}) async-start(), calls=%async_computation.48 | async-start | bytes 2048000 | tf_op jit(solution)/shard_map/all_gather | solution.py:283
  (168 other events, 5729.1 us)
Sparse Core Ops, SparseCore 0:
  246.3 63.0 reduce-scatter.43
  370.9 36.2 reduce-scatter.77
  408.8 37.1 all-gather.70
  503.5 37.1 all-gather.72
  596.8 37.1 all-gather.74
  690.3 37.1 all-gather.76
  783.4 37.1 all-gather.78
  1173.9 54.8 reduce-scatter.35
  1232.6 62.9 reduce-scatter.39
  1299.5 38.7 reduce-scatter.37
  1470.0 36.2 reduce-scatter.57
  1509.1 35.3 reduce-scatter.47
  1583.6 37.1 all-gather.46
  1622.4 37.0 all-gather.36
  1660.9 37.0 all-gather.58
  1775.9 35.3 reduce-scatter.69
  1813.0 37.1 all-gather.48
  1851.8 37.0 all-gather.38
  1890.4 37.0 all-gather.60
  1967.8 35.3 reduce-scatter.51
  2005.4 35.3 reduce-scatter.71
  2042.3 37.1 all-gather.50
  2081.1 37.0 all-gather.40
  2119.7 37.0 all-gather.62
  2234.7 35.3 reduce-scatter.73
  2271.5 37.1 all-gather.52
  2310.2 37.0 all-gather.42
  2348.8 37.0 all-gather.64
  2425.6 35.3 reduce-scatter.55
  2535.9 38.1 all-gather.54
  2575.7 37.4 all-gather.44
  2614.7 37.0 all-gather.66
  (23 shorter events, 716.3 us)
where the time goes:
time: 2680 us; the launch traced here: 2670 us
  waiting for transfers between devices  1540 us (57%)
  matrix products  775 us (29%)
  other arithmetic  119 us (4%)
  local copies, waits for them, and re-layouts  110 us (4%)
  blocking collectives  104 us (4%)
    dot_general x40, matrix products, exact_product(): return jnp.dot(left_side, right_side, precision=lax.Precision.HIGHEST)  214 us
    all_gather x5, waiting for transfers between devices, orthogonalize(): lax.all_gather(gram_pieces[3], 'fsdp', axis=0, tiled=True)  193 us
    reduce_scatter x5, waiting for transfers between devices, orthogonalize(): lax.psum_scatter(exact_gram(current[3]), 'fsdp', scatter_dimension=0, til...  177 us
    all_gather x5, waiting for transfers between devices, orthogonalize(): lax.all_gather(gram_pieces[1], 'fsdp', axis=0, tiled=True)  155 us
    reduce_scatter x5, waiting for transfers between devices, orthogonalize(): lax.psum_scatter(exact_gram(current[0]), 'fsdp', scatter_dimension=0, til...  153 us
    reduce_scatter x5, waiting for transfers between devices, orthogonalize(): lax.psum_scatter(exact_gram(current[2]), 'fsdp', scatter_dimension=0, til...  150 us
    all_gather x5, waiting for transfers between devices, orthogonalize(): lax.all_gather(gram_pieces[0], 'fsdp', axis=0, tiled=True)  114 us
    all_gather x5, waiting for transfers between devices, orthogonalize(): lax.all_gather(gram_pieces[2], 'fsdp', axis=0, tiled=True)  114 us
  transfers between devices with their start and end apart: 55, of which 48 were waited for; matrix products, arithmetic and copies ran while one was open for 20% of the time, Pallas kernels for 0%

commit v1 on v0

v1 whole, which is shorter than its diff:
```python
import functools
import math

import jax
import jax.numpy as jnp
from jax import lax
from jax.experimental import pallas as pl
from jax.experimental.pallas import tpu as pltpu
from jax.sharding import PartitionSpec as P

HEAD_DIM = 32
NS_ITERS = 5
STEP = 10
LANES = 128
LONGEST = 768

norm_eps = 1e-05
masked_score = -1e30
poly_linear = 3.4445
poly_square = -4.775
poly_cubic = 2.0315
muon_rate = 0.5
muon_decay = 0.01
moment_keep = 0.5
adam_rate = 0.05
beta_first = 0.9
beta_second = 0.999
adam_eps = 1e-08


def layer_norm(values, gain_row, shift_row):
    center = values - jnp.mean(values, axis=-1, keepdims=True)
    spread = jnp.mean(center * center, axis=-1, keepdims=True)
    return center * lax.rsqrt(spread + norm_eps) * gain_row + shift_row


def gelu_exact(values):
    return 0.5 * values * (1.0 + lax.erf(values * (1.0 / math.sqrt(2.0))))


def nn(left, right):
    return jnp.dot(left, right, preferred_element_type=jnp.float32)


def nt(left, right):
    return lax.dot_general(left, right, (((1,), (1,)), ((), ())), preferred_element_type=jnp.float32)


def tn(left, right):
    return lax.dot_general(left, right, (((0,), (0,)), ((), ())), preferred_element_type=jnp.float32)


def _half_mask(shape):
    lane = lax.broadcasted_iota(jnp.int32, shape, 1)
    return (lane % HEAD_DIM) < (HEAD_DIM // 2)


def _turn(values, first):
    half = HEAD_DIM // 2
    left = pltpu.roll(values, LANES - half, 1)
    right = pltpu.roll(values, half, 1)
    return jnp.where(first, left, right)


def attention_forward_kernel(
    q_ref, k_ref, v_ref, cos_ref, sin_ref, segc_ref, segr_ref,
    qr_ref, kr_ref, vr_ref, attn_ref, lse_ref,
    qt_s, vt_s, ot_s,
):
    first = _half_mask(cos_ref.shape)
    cosine, sine = cos_ref[...], sin_ref[...]
    queries = q_ref[...] * (1.0 / math.sqrt(HEAD_DIM))
    qr = (queries * cosine + _turn(queries, first) * sine).astype(jnp.bfloat16)
    keys = k_ref[...]
    kr = (keys * cosine + _turn(keys, first) * sine).astype(jnp.bfloat16)
    vr = v_ref[...].astype(jnp.bfloat16)
    qr_ref[...] = qr
    kr_ref[...] = kr
    vr_ref[...] = vr
    qt_s[...] = qr.T
    vt_s[...] = vr.T
    tokens = qr.shape[0]
    rest = tokens - LONGEST
    row = lax.broadcasted_iota(jnp.int32, (LANES, tokens), 0)
    same = segc_ref[LONGEST:, :] == segr_ref[:, LONGEST:]

    def head(h, carry):
        qth = jnp.where(row // HEAD_DIM == h, qt_s[...], jnp.zeros((), jnp.bfloat16))
        rows = pl.ds(pl.multiple_of(h * HEAD_DIM, HEAD_DIM), HEAD_DIM)

        def block(start, width, key_start, key_count, mask):
            scores = nn(kr_ref[key_start : key_start + key_count, :], qth[:, start : start + width])
            if mask is not None:
                scores = jnp.where(mask, scores, masked_score)
            peak = jnp.max(scores, axis=0, keepdims=True)
            raised = jnp.exp(scores - peak)
            total = jnp.sum(raised, axis=0, keepdims=True)
            out = nn(vt_s[rows, key_start : key_start + key_count], raised.astype(jnp.bfloat16))
            ot_s[rows, start : start + width] = out / total
            lse_ref[0, pl.ds(h, 1), start : start + width] = peak + jnp.log(total)

        for start in range(0, LONGEST, 256):
            block(start, 256, 0, LONGEST, None)
        block(LONGEST, rest, LONGEST, rest, same)
        return carry

    lax.fori_loop(0, LANES // HEAD_DIM, head, 0)
    attn_ref[...] = ot_s[...].T.astype(jnp.bfloat16)


def attention_forward(project, cosine, sine, seg_col, seg_row):
    tokens = project.shape[0]
    width = project.shape[1] // 3
    groups = width // LANES
    col = lambda shift: pl.BlockSpec((tokens, LANES), lambda g, shift=shift: (0, g + shift))
    whole = lambda shape: pl.BlockSpec(shape, lambda g: (0,) * len(shape))
    flops = 4 * (LONGEST**2 + (tokens - LONGEST) ** 2) * 128 * groups * 4
    return pl.pallas_call(
        attention_forward_kernel,
        grid=(groups,),
        in_specs=[col(0), col(groups), col(2 * groups), whole((tokens, LANES)), whole((tokens, LANES)),
                  whole((tokens, 1)), whole((1, tokens))],
        out_specs=[col(0)] * 4 + [pl.BlockSpec((1, 4, tokens), lambda g: (g, 0, 0))],
        out_shape=[jax.ShapeDtypeStruct((tokens, width), jnp.bfloat16)] * 4
        + [jax.ShapeDtypeStruct((groups, 4, tokens), jnp.float32)],
        scratch_shapes=[
            pltpu.VMEM((LANES, tokens), jnp.bfloat16),
            pltpu.VMEM((LANES, tokens), jnp.bfloat16),
            pltpu.VMEM((LANES, tokens), jnp.float32),
        ],
        compiler_params=pltpu.CompilerParams(vmem_limit_bytes=48 << 20),
        cost_estimate=pl.CostEstimate(flops=flops, bytes_accessed=20 << 20, transcendentals=20 << 20),
        name="attention_forward",
    )(project, project, project, cosine, sine, seg_col, seg_row)


def attention_backward_kernel(
    qr_ref, kr_ref, vr_ref, do_ref, attn_ref, lse_ref, cos_ref, sin_ref, segc_ref, segr_ref,
    dq_ref, dk_ref, dv_ref,
    qt_s, dot_s, kt_s, delta_s, dqt_s, dk_s, dv_s,
):
    tokens = qr_ref.shape[0]
    rest = tokens - LONGEST
    qt_s[...] = qr_ref[...].T
    dot_s[...] = do_ref[...].T
    kt_s[...] = kr_ref[...].T
    prod_t = (do_ref[...].astype(jnp.float32) * attn_ref[...].astype(jnp.float32)).T
    for h in range(4):
        delta_s[h : h + 1, :] = jnp.sum(prod_t[h * HEAD_DIM : (h + 1) * HEAD_DIM, :], axis=0, keepdims=True)
    dk_s[...] = jnp.zeros_like(dk_s)
    dv_s[...] = jnp.zeros_like(dv_s)
    row = lax.broadcasted_iota(jnp.int32, (LANES, tokens), 0)
    lane = lax.broadcasted_iota(jnp.int32, (tokens, LANES), 1)
    same = segc_ref[LONGEST:, :] == segr_ref[:, LONGEST:]
    zero = jnp.zeros((), jnp.bfloat16)

    def head(h, carry):
        mine_t = row // HEAD_DIM == h
        mine = lane // HEAD_DIM == h
        qth = jnp.where(mine_t, qt_s[...], zero)
        doth = jnp.where(mine_t, dot_s[...], zero)
        qh = jnp.where(mine, qr_ref[...], zero)
        doh = jnp.where(mine, do_ref[...], zero)
        rows = pl.ds(pl.multiple_of(h * HEAD_DIM, HEAD_DIM), HEAD_DIM)

        def block(start, width, key_start, key_count, mask):
            at = slice(start, start + width)
            keys = slice(key_start, key_start + key_count)
            scores = nn(kr_ref[keys, :], qth[:, at])
            if mask is not None:
                scores = jnp.where(mask, scores, masked_score)
            soft = jnp.exp(scores - lse_ref[0, pl.ds(h, 1), at])
            weight_grad = nn(vr_ref[keys, :], doth[:, at])
            score_grad = (soft * (weight_grad - delta_s[pl.ds(h, 1), at])).astype(jnp.bfloat16)
            dv_s[keys, :] += nn(soft.astype(jnp.bfloat16), doh[at, :])
            dk_s[keys, :] += nn(score_grad, qh[at, :])
            dqt_s[rows, at] = nn(kt_s[rows, keys], score_grad)

        for start in range(0, LONGEST, 256):
            block(start, 256, 0, LONGEST, None)
        block(LONGEST, rest, LONGEST, rest, same)
        return carry

    lax.fori_loop(0, LANES // HEAD_DIM, head, 0)
    first = _half_mask(cos_ref.shape)
    cosine, sine = cos_ref[...], sin_ref[...]

    def pull(values):
        return values * cosine + _turn(values * sine, first)

    dq_ref[...] = (pull(dqt_s[...].T) * (1.0 / math.sqrt(HEAD_DIM))).astype(jnp.bfloat16)
    dk_ref[...] = pull(dk_s[...]).astype(jnp.bfloat16)
    dv_ref[...] = dv_s[...].astype(jnp.bfloat16)


def attention_backward(qr, kr, vr, attn_grad, attn, lse, cosine, sine, seg_col, seg_row):
    tokens, width = qr.shape
    groups = width // LANES
    col = pl.BlockSpec((tokens, LANES), lambda g: (0, g))
    whole = lambda shape: pl.BlockSpec(shape, lambda g: (0,) * len(shape))
    flops = 10 * (LONGEST**2 + (tokens - LONGEST) ** 2) * 128 * groups * 4
    return pl.pallas_call(
        attention_backward_kernel,
        grid=(groups,),
        in_specs=[col] * 5 + [pl.BlockSpec((1, 4, tokens), lambda g: (g, 0, 0)),
                              whole((tokens, LANES)), whole((tokens, LANES)), whole((tokens, 1)), whole((1, tokens))],
        out_specs=[col] * 3,
        out_shape=[jax.ShapeDtypeStruct((tokens, width), jnp.bfloat16)] * 3,
        scratch_shapes=[
            pltpu.VMEM((LANES, tokens), jnp.bfloat16),
            pltpu.VMEM((LANES, tokens), jnp.bfloat16),
            pltpu.VMEM((LANES, tokens), jnp.bfloat16),
            pltpu.VMEM((8, tokens), jnp.float32),
            pltpu.VMEM((LANES, tokens), jnp.float32),
            pltpu.VMEM((tokens, LANES), jnp.float32),
            pltpu.VMEM((tokens, LANES), jnp.float32),
        ],
        compiler_params=pltpu.CompilerParams(vmem_limit_bytes=48 << 20),
        cost_estimate=pl.CostEstimate(flops=flops, bytes_accessed=20 << 20, transcendentals=20 << 20),
        name="attention_backward",
    )(qr, kr, vr, attn_grad, attn, lse, cosine, sine, seg_col, seg_row)


def row_layout(lengths, counts, row_len):
    lens = lengths[0]
    slots = lens.shape[0]
    order = lax.broadcasted_iota(jnp.int32, (slots, slots), 0)
    upto = lax.broadcasted_iota(jnp.int32, (slots, slots), 1)
    starting = jnp.sum(jnp.where(upto < order, lens[None, :], 0), axis=1)
    slot = lax.broadcasted_iota(jnp.int32, (slots,), 0)
    which = jnp.min(jnp.where(lens == LONGEST, slot, slots))
    offset = jnp.sum(jnp.where(slot == which, starting, 0))
    places = lax.broadcasted_iota(jnp.int32, (row_len,), 0) + offset
    places = jnp.where(places >= row_len, places - row_len, places)
    endings = starting + lens
    segment = jnp.sum((places[:, None] >= endings[None, :]).astype(jnp.int32), axis=1)
    member = segment[:, None] == slot[None, :]
    first_place = jnp.sum(jnp.where(member, starting[None, :], 0), axis=1)
    position = (places - first_place).astype(jnp.float32)
    inverse_count = 1.0 / counts[0].astype(jnp.float32)
    share = jnp.sum(jnp.where(member, inverse_count[None, :], 0.0), axis=1)
    return offset, segment, position, share


def rotary_tables(position):
    lane = lax.broadcasted_iota(jnp.int32, (1, LANES), 1)
    indices = (lane % (HEAD_DIM // 2)).astype(jnp.float32)
    inverse = jnp.exp(indices * (-2.0 * math.log(10000.0) / HEAD_DIM))
    angles = position[:, None] * inverse
    sign = jnp.where((lane % HEAD_DIM) < (HEAD_DIM // 2), -1.0, 1.0)
    return jnp.cos(angles), jnp.sin(angles) * sign


def turn_rows(values, shift):
    twice = jnp.concatenate([values, values], axis=0)
    return lax.dynamic_slice_in_dim(twice, shift, values.shape[0], 0)


def high(left, right):
    return jnp.dot(left, right, precision=lax.Precision.HIGH, preferred_element_type=jnp.float32)


def shards(
    tokens, cotangent, lengths, counts,
    w_qkv, w_out, w_up, w_down,
    mom_qkv, mom_out, mom_up, mom_down,
    vectors, vec_first, vec_second,
):
    both = ("fsdp", "dp")
    planes = lax.axis_size("fsdp")
    ranks = lax.axis_size("dp")
    row_len, width = tokens.shape
    columns = w_qkv.shape[1]
    old_weights = (w_qkv, w_out, w_up, w_down)
    old_moments = (mom_qkv, mom_out, mom_up, mom_down)
    counts_rows = [w.shape[0] for w in old_weights]
    n_vec = vectors.shape[0]

    slab_a = jnp.concatenate([w_qkv.T, w_out.T, vectors.T], axis=1).astype(jnp.bfloat16)
    slab_b = jnp.concatenate([w_up.T, w_down.T], axis=1).astype(jnp.bfloat16)
    full_a = lax.all_gather(slab_a, both, axis=0, tiled=True).reshape(planes, width, -1)
    full_b = lax.all_gather(slab_b, both, axis=0, tiled=True).reshape(planes, width, -1)
    r0, r1, r2, r3 = counts_rows
    wt_qkv = jnp.concatenate([full_a[j, :, :r0] for j in range(planes)], axis=1)
    wt_out = jnp.concatenate([full_a[j, :, r0 : r0 + r1] for j in range(planes)], axis=1)
    table = full_a[0, :, r0 + r1 :].T.astype(jnp.float32)
    wt_up = jnp.concatenate([full_b[j, :, :r2] for j in range(planes)], axis=1)
    wt_down = jnp.concatenate([full_b[j, :, r2:] for j in range(planes)], axis=1)

    offset, segment, position, share = row_layout(lengths, counts, row_len)
    cosine, sine = rotary_tables(position)
    seg_col, seg_row = segment[:, None], segment[None, :]
    inputs = turn_rows(tokens, offset).astype(jnp.float32)
    incoming = turn_rows(cotangent, offset).astype(jnp.float32) * share[:, None]

    normed_one, pull_one = jax.vjp(layer_norm, inputs, table[0], table[1])
    normed_one = normed_one.astype(jnp.bfloat16)
    project = nn(normed_one, wt_qkv) + table[4:7].reshape(-1)
    qr, kr, vr, attn, lse = attention_forward(project, cosine, sine, seg_col, seg_row)
    after = inputs + (nn(attn, wt_out) + table[7])
    normed_two, pull_two = jax.vjp(layer_norm, after, table[2], table[3])
    normed_two = normed_two.astype(jnp.bfloat16)
    hidden_pre = nn(normed_two, wt_up) + table[9:].reshape(-1)
    hidden, pull_hidden = jax.vjp(gelu_exact, hidden_pre)
    hidden = hidden.astype(jnp.bfloat16)
    layer_out = (after + (nt(hidden, wt_down) + table[8])).astype(jnp.bfloat16)

    grad_low = incoming.astype(jnp.bfloat16)
    grad_t_down = tn(grad_low, hidden)
    pre_grad = pull_hidden(nn(grad_low, wt_down))[0].astype(jnp.bfloat16)
    grad_t_up = tn(normed_two, pre_grad)
    resid_grad, gain_two, shift_two = pull_two(nt(pre_grad, wt_up))
    after_grad = incoming + resid_grad
    branch_low = after_grad.astype(jnp.bfloat16)
    grad_t_out = tn(attn, branch_low)
    attn_grad = nt(branch_low, wt_out).astype(jnp.bfloat16)
    dq, dk, dv = attention_backward(qr, kr, vr, attn_grad, attn, lse, cosine, sine, seg_col, seg_row)
    proj_grad = jnp.concatenate([dq, dk, dv], axis=1)
    grad_t_qkv = tn(normed_one, proj_grad)
    in_grad, gain_one, shift_one = pull_one(nt(proj_grad, wt_qkv))
    input_grad = after_grad + in_grad

    def column_sum(values):
        return jnp.sum(values.astype(jnp.float32), axis=0)

    vector_grad = jnp.concatenate(
        [gain_one[None], shift_one[None], gain_two[None], shift_two[None],
         column_sum(proj_grad).reshape(3, width), column_sum(branch_low)[None], column_sum(grad_low)[None],
         column_sum(pre_grad).reshape(-1, width)],
        axis=0,
    )
    back = jnp.where(offset > 0, row_len - offset, 0)
    layer_out = turn_rows(layer_out, back)
    input_grad = turn_rows(input_grad, back)

    def cut(values, j, rows):
        return values[:, j * rows : (j + 1) * rows]

    parts_b = jnp.stack([jnp.concatenate([cut(grad_t_up, j, r2), cut(grad_t_down, j, r3)], axis=1) for j in range(planes)])
    own_b = lax.psum_scatter(parts_b.reshape(planes * width, -1), both, scatter_dimension=0, tiled=True)
    parts_a = jnp.stack([jnp.concatenate([cut(grad_t_qkv, j, r0), cut(grad_t_out, j, r1), vector_grad.T], axis=1) for j in range(planes)])
    own_a = lax.psum_scatter(parts_a.reshape(planes * width, -1), both, scatter_dimension=0, tiled=True)
    grads_t = (own_a[:, :r0], own_a[:, r0 : r0 + r1], own_b[:, :r2], own_b[:, r2:])
    vector_grad = own_a[:, r0 + r1 :].T
    new_moments_t = [moment_keep * old.T + grad for old, grad in zip(old_moments, grads_t)]

    most = max(counts_rows)
    padded = [jnp.pad(m.astype(jnp.bfloat16), ((0, 0), (0, most - m.shape[1]))) for m in new_moments_t]
    sent = jnp.stack([padded[t % 4] for t in range(planes)])
    mine = lax.all_to_all(sent, "fsdp", 0, 0, tiled=True)
    mine = mine.transpose(1, 0, 2).reshape(columns, planes * most)
    whole = lax.all_gather(mine, "dp", axis=0, tiled=True)
    gram = nt(whole, whole)
    identity = jnp.eye(width, dtype=jnp.float32)
    norm_sq = jnp.trace(gram) + 1e-07
    gram = gram / norm_sq
    factor = None
    for iteration in range(NS_ITERS):
        poly = poly_linear * identity + poly_square * gram + poly_cubic * high(gram, gram)
        factor = poly if factor is None else high(factor, poly)
        if iteration + 1 < NS_ITERS:
            gram = high(high(gram, poly), poly)
    own_rows = lax.dynamic_slice_in_dim(factor, lax.axis_index("dp") * columns, columns, 0) * lax.rsqrt(norm_sq)
    own_orth = high(own_rows, whole.astype(jnp.float32))
    own_orth = own_orth.astype(jnp.bfloat16).reshape(columns, planes, most).transpose(1, 0, 2)
    pieces = lax.all_to_all(own_orth, "fsdp", 0, 0, tiled=True).astype(jnp.float32)

    new_weights = []
    for x, weight_old in enumerate(old_weights):
        rows = weight_old.shape[0]
        scale = muon_rate * math.sqrt(max(1.0, rows * planes / width))
        new_weights.append(weight_old * (1.0 - muon_rate * muon_decay) - scale * pieces[x, :, :rows].T)
    new_first = beta_first * vec_first + (1.0 - beta_first) * vector_grad
    new_second = beta_second * vec_second + (1.0 - beta_second) * vector_grad * vector_grad
    first_fix = 1.0 - beta_first**STEP
    second_fix = 1.0 - beta_second**STEP
    new_vectors = vectors - adam_rate * (new_first / first_fix) / (jnp.sqrt(new_second / second_fix) + adam_eps)
    return (layer_out, input_grad, *[m.T for m in new_moments_t], *new_weights, new_vectors, new_first, new_second)


def solution(mesh):
    rows, cells, table = P(("dp", "fsdp"), None), P("fsdp", "dp"), P(None, "dp")
    return jax.shard_map(
        shards,
        mesh=mesh,
        in_specs=(rows,) * 4 + (cells,) * 8 + (table,) * 3,
        out_specs=(rows,) * 2 + (cells,) * 8 + (table,) * 3,
        check_vma=False,
    )
```

time: 2680 us -> 672 us (0.25)
  waiting for transfers between devices: 1540 us -> 323 us
  matrix products: 775 us -> 124 us
  blocking collectives: 104 us -> 11.4 us
  Pallas kernels: 0 us -> 89.5 us
  local copies, waits for them, and re-layouts: 110 us -> 38.3 us
  other arithmetic: 119 us -> 55.6 us
    dot_general x253 -> x31, matrix products: 775 us -> 124 us  [the longest x18 43.9 us: high(): jnp.dot(left, right, precision=lax.Precision.HIGH, preferred_element_type...]
    all_gather x26 -> x3, waiting for transfers between devices: 666 us -> 68.3 us  [the longest x1 47.7 us: shards(): lax.all_gather(slab_a, both, axis=0, tiled=True).reshape(planes, width, -1)]
    reduce_scatter x27 -> x2, waiting for transfers between devices: 841 us -> 254 us  [the longest x1 155 us: shards(): lax.psum_scatter(parts_b.reshape(planes * width, -1), both, scatter_dimen...]
    all_gather x7 -> x0, blocking collectives: 93.3 us -> none  [the longest x1 16.3 us: shards(): lax.all_gather(w_up.astype(jnp.bfloat16), 'fsdp', axis=0, tiled=True)]
    pallas_call x0 -> x2, Pallas kernels: none -> 89.5 us  [the longest x1 47.1 us: attention_forward(): pl.pallas_call(attention_forward_kernel, grid=(groups,), in_specs=[col(0)...]
    unnamed x223 -> x96, local copies, waits for them, and re-layouts: 56.1 us -> 10.6 us
    reduce_sum x49 -> x8, other arithmetic: 48.5 us -> 5.66 us  [the longest x3 3.3 us: column_sum(): return jnp.sum(values.astype(jnp.float32), axis=0)]
    while x80 -> x0, local copies, waits for them, and re-layouts: 29.3 us -> none
  transfers between devices with their start and end apart: 55 -> 6, of which waited for: 48 -> 5; matrix products, arithmetic and copies ran while one was open for 20% -> 12% of each run, Pallas kernels for 0% -> 7%
where the time goes in v1:
time: 672 us; the launch traced here: 666 us
  waiting for transfers between devices  323 us (48%)
  matrix products  124 us (18%)
  Pallas kernels  89.5 us (13%)
  other arithmetic  55.6 us (8%)
  local copies, waits for them, and re-layouts  38.3 us (6%)
  between operations  19 us (3%)
  blocking collectives  11.4 us (2%)
    reduce_scatter x1, waiting for transfers between devices, shards(): lax.psum_scatter(parts_b.reshape(planes * width, -1), both, scatter_dimen...  155 us
    reduce_scatter x1, waiting for transfers between devices, shards(): lax.psum_scatter(parts_a.reshape(planes * width, -1), both, scatter_dimen...  98.5 us
    all_gather x1, waiting for transfers between devices, shards(): lax.all_gather(slab_a, both, axis=0, tiled=True).reshape(planes, width, -1)  47.7 us
    pallas_call x1, Pallas kernels, attention_forward(): pl.pallas_call(attention_forward_kernel, grid=(groups,), in_specs=[col(0)...  47.1 us
    dot_general x18, matrix products, high(): jnp.dot(left, right, precision=lax.Precision.HIGH, preferred_element_type...  43.9 us
    pallas_call x1, Pallas kernels, attention_backward(): pl.pallas_call(attention_backward_kernel, grid=(groups,), in_specs=[col]...  42.4 us
    dot_general x4, matrix products, nn(): return jnp.dot(left, right, preferred_element_type=jnp.float32)  33.7 us
    dot_general x5, matrix products, nt(): lax.dot_general(left, right, (((1,), (1,)), ((), ())), preferred_element_...  27 us
  transfers between devices with their start and end apart: 6, of which 5 were waited for; matrix products, arithmetic and copies ran while one was open for 12% of the time, Pallas kernels for 7%

profile of v1, /device:TPU:0, one launch (start us, length us, event | category | flops | bytes accessed | tf_op | source)
XLA Modules:
  0.0 666.2 jit_solution(7695430212036242345)
XLA Ops:
  27.7 47.7 %all-gather.4.cloned.1.call-done = bf16[2560,653]{1,0:T(8,128)(2,1)} async-done(((bf16[80,653]{1,0:T(8,128)(2,1)}), bf16[2560,653]{1,0:T(8,128)(2,1)}) %all-gather.4.cloned.1.call-update) | async-done | bytes 3343376 | tf_op jit(solution)/shard_map/all_gather | solution.py:281
  76.5 2.9 slice_bitcast_fusion.8
  79.5 5.2 concatenate.64
  87.5 7.8 %broadcast_add_fusion.q_ref.k_ref.v_ref = f32[1024,1920]{1,0:T(8,128)} fusion(f32[1920]{0:T(1024)S(1)} %add.224, bf16[640,1920]{1,0:T(8,128)(2,1)} %concatenate.64, bf16[1024,640]{1,0:T(8,128)(2,1)S(1)} %copy-done.11, f32[640]{0:T(1024)S(1)} %get-tuple-element.118, f32[640]{0:T(1024)S(1)} %get-tuple-element.119, f32[1024]{0:T(1024)S(1)} %fusion.55, ...), kind=kOutput, calls=%fused_computation.15 | convolution fusion | flops 2522480640 | bytes 11653632 | tf_op jit(solution)/shard_map/dot_general | solution.py:42
  95.3 47.1 %attention_forward.1 = (bf16[1024,640]{1,0:T(8,128)(2,1)S(1)}, bf16[1024,640]{1,0:T(8,128)(2,1)S(1)}, bf16[1024,640]{1,0:T(8,128)(2,1)S(1)}, bf16[1024,640]{1,0:T(8,128)(2,1)}, f32[5,4,1024]{2,1,0:T(4,128)S(1)}) custom-call(f32[1024,1920]{1,0:T(8,128)} %broadcast_add_fusion.q_ref.k_ref.v_ref, f32[1024,1920]{1,0:T(8,128)} %broadcast_add_fusion.q_ref.k_ref.v_ref, ...), custom_call_target="tpu_custom_call" | custom-call | flops 6710886400 | bytes 20971520 | tf_op jit(solution)/shard_map/attention_forward/pallas_call | solution.py:118
  142.4 3.9 fusion.91
  148.3 3.6 slice_bitcast_fusion.3
  152.0 9.7 %multiply_convert_fusion = (bf16[1024,2560]{1,0:T(8,128)(2,1)}, f32[1024,2560]{1,0:T(8,128)}) fusion(f32[2560]{0:T(1024)S(1)} %add.240, bf16[640,640]{1,0:T(8,128)(2,1)S(1)} %get-tuple-element.143, bf16[640,640]{1,0:T(8,128)(2,1)S(1)} %get-tuple-element.144, bf16[640,640]{1,0:T(8,128)(2,1)S(1)} %get-tuple-element.145, ...), kind=kOutput, calls=%fused_computation.3 | convolution fusion | flops 3387555840 | bytes 21650432 | tf_op jit(solution)/shard_map/dot_general | solution.py:42
  161.7 12.3 %convert_reduce_fusion = (f32[2560]{0:T(1024)S(1)}, bf16[1024,2560]{1,0:T(8,128)(2,1)S(1)}) fusion(bf16[640,640]{1,0:T(8,128)(2,1)S(1)} %get-tuple-element.140, bf16[640,640]{1,0:T(8,128)(2,1)S(1)} %get-tuple-element.141, bf16[640,640]{1,0:T(8,128)(2,1)S(1)} %get-tuple-element.142, bf16[640,640]{1,0:T(8,128)(2,1)S(1)} %get-tuple-element.139, ...), kind=kOutput, calls=%fused_computation.1 | convolution fusion | flops 3412456960 | bytes 20340736 | tf_op jit(solution)/shard_map/dot_general | solution.py:42
  174.1 4.6 multiply_reduce_fusion
  186.7 42.4 %attention_backward.1 = (bf16[1024,640]{1,0:T(8,128)(2,1)S(1)}, bf16[1024,640]{1,0:T(8,128)(2,1)S(1)}, bf16[1024,640]{1,0:T(8,128)(2,1)S(1)}) custom-call(bf16[1024,640]{1,0:T(8,128)(2,1)} %copy-done, bf16[1024,640]{1,0:T(8,128)(2,1)} %copy-done.1, bf16[1024,640]{1,0:T(8,128)(2,1)} %copy-done.2, bf16[1024,640]{1,0:T(8,128)(2,1)} %convolution_convert_fusion.1.do_ref, ...), custom_call_target="tpu_custom_call" | custom-call | flops 16777216000 | bytes 20971520 | tf_op jit(solution)/shard_map/attention_backward/pallas_call | solution.py:202
  231.8 4.9 fusion.80
  236.7 4.9 fusion.75
  241.6 3.6 fusion.90
  245.3 3.3 fusion.8
  249.5 3.9 fusion.89
  253.4 2.8 fusion.13
  256.3 3.8 pad_maximum_fusion.1
  261.9 6.1 fusion.79
  269.3 5.9 fusion.72
  276.7 5.3 pad_maximum_fusion
  282.9 98.5 %reduce-scatter.7.cloned.1.call-done = f32[80,653]{1,0:T(8,128)} async-done(((f32[2560,653]{1,0:T(8,128)}), f32[80,653]{1,0:T(8,128)}) %reduce-scatter.7.cloned.1.call-update) | async-done | bytes 208976 | tf_op jit(solution)/shard_map/reduce_scatter | solution.py:342
  385.4 155.2 %reduce-scatter.9.cloned.1.call-done = f32[80,1280]{1,0:T(8,128)} async-done(((f32[2560,1280]{1,0:T(8,128)}), f32[80,1280]{1,0:T(8,128)}) %reduce-scatter.9.cloned.1.call-update) | async-done | bytes 409616 | tf_op jit(solution)/shard_map/reduce_scatter | solution.py:340
  543.6 11.4 %all_to_all.10 = bf16[4,80,640]{2,1,0:T(8,128)(2,1)S(1)} all-to-all(bf16[4,80,640]{2,1,0:T(8,128)(2,1)S(1)} %pad_maximum_fusion.13), channel_id=1, replica_groups=mesh['dp'=8,'fsdp'=4] {'fsdp'}, dimensions={0} | all-to-all | bytes 819200 | tf_op jit(solution)/shard_map/all_to_all | solution.py:350
  558.9 8.6 %add_convert_fusion.1 = bf16[1024,640]{1,0:T(8,128)(2,1)} fusion(f32[1024,640]{1,0:T(8,128)S(1)} %copy-done.5, bf16[1024,2560]{1,0:T(8,128)(2,1)} %get-tuple-element.183, f32[640]{0:T(1024)} %get-tuple-element.114, bf16[640,640]{1,0:T(8,128)(2,1)} %copy-done.20, bf16[640,640]{1,0:T(8,128)(2,1)} %copy-done.21, bf16[640,640]{1,0:T(8,128)(2,1)} %copy-done.22, ...), kind=kOutput, calls=%fused_computation.57 | convolution fusion | flops 3370516480 | bytes 12454400 | tf_op jit(solution)/shard_map/dot_general | solution.py:46
  567.5 20.6 %all-gather.8.cloned.1.call-done = bf16[640,2560]{1,0:T(8,128)(2,1)} async-done(((bf16[80,2560]{1,0:T(8,128)(2,1)}), bf16[640,2560]{1,0:T(8,128)(2,1)}) %all-gather.8.cloned.1.call-update) | async-done | bytes 3276816 | tf_op jit(solution)/shard_map/all_gather | solution.py:352
  588.1 6.3 select_reduce_fusion
  627.5 2.9 fusion.102
  639.9 4.8 all-to-all-start.1
  644.7 3.3 add_add_fusion.2
  648.1 3.4 fusion.28
  651.5 2.8 fusion.11
  (203 shorter events, 97.7 us)
Async XLA Ops:
  7.2 12.7 %copy-start.42 = (s32[1,4]{1,0:T(1,128)S(1)}, s32[1,4]{1,0:T(1,128)}, u32[]{:S(2)}) copy-start(s32[1,4]{1,0:T(1,128)} %param.18) | copy-start | bytes 52
  7.2 12.8 %copy-start.16 = (bf16[1024,640]{1,0:T(8,128)(2,1)S(1)}, bf16[1024,640]{1,0:T(8,128)(2,1)}, u32[]{:S(2)}) copy-start(bf16[1024,640]{1,0:T(8,128)(2,1)} %param.16) | copy-start | bytes 3932164
  7.2 68.2 %all-gather.4.cloned.1.call-start = ((), (), s32[]{:S(2)}) async-start(), calls=%async_computation.4 | async-start | bytes 4055040 | tf_op jit(solution)/shard_map/all_gather | solution.py:281
  10.9 137.4 %all-gather.6.cloned.1.call-start = ((), (), s32[]{:S(2)}) async-start(), calls=%async_computation.5 | async-start | bytes 6758400 | tf_op jit(solution)/shard_map/all_gather | solution.py:282
  12.7 368.8 %reduce-scatter.7.cloned.1.call-start = ((), (), s32[]{:S(2)}) async-start(), calls=%async_computation.7 | async-start | bytes 8110080 | tf_op jit(solution)/shard_map/reduce_scatter | solution.py:342
  25.8 219.4 %copy-start.35 = (f32[1024]{0:T(1024)}, f32[1024]{0:T(1024)S(1)}, u32[]{:S(2)}) copy-start(f32[1024]{0:T(1024)S(1)} %fusion.55) | copy-start | bytes 12292
  87.5 54.9 %copy-start.26 = (bf16[640,160]{1,0:T(8,128)(2,1)}, bf16[640,160]{1,0:T(8,128)(2,1)S(1)}, u32[]{:S(2)}) copy-start(bf16[640,160]{1,0:T(8,128)(2,1)S(1)} %get-tuple-element.153) | copy-start | bytes 614404
  87.5 54.9 %copy-start.28 = (bf16[640,160]{1,0:T(8,128)(2,1)}, bf16[640,160]{1,0:T(8,128)(2,1)S(1)}, u32[]{:S(2)}) copy-start(bf16[640,160]{1,0:T(8,128)(2,1)S(1)} %get-tuple-element.154) | copy-start | bytes 614404
  142.3 3.9 copy-start
  142.3 3.9 copy-start.1
  142.3 3.9 copy-start.2
  148.3 3.7 copy-start.4
  151.9 9.8 %copy-start.18 = (bf16[640,640]{1,0:T(8,128)(2,1)}, bf16[640,640]{1,0:T(8,128)(2,1)S(1)}, u32[]{:S(2)}) copy-start(bf16[640,640]{1,0:T(8,128)(2,1)S(1)} %get-tuple-element.139) | copy-start | bytes 2457604
  151.9 9.8 %copy-start.20 = (bf16[640,640]{1,0:T(8,128)(2,1)}, bf16[640,640]{1,0:T(8,128)(2,1)S(1)}, u32[]{:S(2)}) copy-start(bf16[640,640]{1,0:T(8,128)(2,1)S(1)} %get-tuple-element.140) | copy-start | bytes 2457604
  151.9 9.8 %copy-start.21 = (bf16[640,640]{1,0:T(8,128)(2,1)}, bf16[640,640]{1,0:T(8,128)(2,1)S(1)}, u32[]{:S(2)}) copy-start(bf16[640,640]{1,0:T(8,128)(2,1)S(1)} %get-tuple-element.141) | copy-start | bytes 2457604
  151.9 9.8 %copy-start.22 = (bf16[640,640]{1,0:T(8,128)(2,1)}, bf16[640,640]{1,0:T(8,128)(2,1)S(1)}, u32[]{:S(2)}) copy-start(bf16[640,640]{1,0:T(8,128)(2,1)S(1)} %get-tuple-element.142) | copy-start | bytes 2457604
  152.0 9.7 %copy-start.8 = (bf16[1024,640]{1,0:T(8,128)(2,1)S(1)}, bf16[1024,640]{1,0:T(8,128)(2,1)}, u32[]{:S(2)}) copy-start(bf16[1024,640]{1,0:T(8,128)(2,1)} %get-tuple-element.124) | copy-start | bytes 3932164
  174.1 4.6 copy-start.13
  260.2 280.4 %reduce-scatter.9.cloned.1.call-start = ((), (), s32[]{:S(2)}) async-start(), calls=%async_computation.8 | async-start | bytes 13516800 | tf_op jit(solution)/shard_map/reduce_scatter | solution.py:340
  282.0 99.5 %copy-start.31 = (f32[480,80]{0,1:T(8,128)S(1)}, f32[480,80]{0,1:T(8,128)}, u32[]{:S(2)}) copy-start(f32[480,80]{0,1:T(8,128)} %param.23) | copy-start | bytes 460804
  282.0 306.1 %all-gather.8.cloned.1.call-start = ((), (), s32[]{:S(2)}) async-start(), calls=%async_computation.6 | async-start | bytes 3686400 | tf_op jit(solution)/shard_map/all_gather | solution.py:352
  383.7 175.2 %copy-start.19 = (bf16[640,640]{1,0:T(8,128)(2,1)S(1)}, bf16[640,640]{1,0:T(8,128)(2,1)}, u32[]{:S(2)}) copy-start(bf16[640,640]{1,0:T(8,128)(2,1)} %copy-done.18) | copy-start | bytes 2457604
  637.8 6.9 %copy-start.7 = (f32[1024,640]{1,0:T(8,128)S(1)}, f32[1024,640]{1,0:T(8,128)}, u32[]{:S(2)}) copy-start(f32[1024,640]{1,0:T(8,128)} %copy-done.6) | copy-start | bytes 7864324
  637.8 6.9 %copy-start.34 = (f32[1024]{0:T(1024)S(1)}, f32[1024]{0:T(1024)}, u32[]{:S(2)}) copy-start(f32[1024]{0:T(1024)} %copy-done.33) | copy-start | bytes 12292
  637.8 6.9 %copy-start.36 = (f32[1024]{0:T(1024)S(1)}, f32[1024]{0:T(1024)}, u32[]{:S(2)}) copy-start(f32[1024]{0:T(1024)} %copy-done.35) | copy-start | bytes 12292
  637.8 6.9 %copy-start.38 = (f32[1024]{0:T(1024)S(1)}, f32[1024]{0:T(1024)}, u32[]{:S(2)}) copy-start(f32[1024]{0:T(1024)} %copy-done.37) | copy-start | bytes 12292
  639.9 17.2 %all-to-all-start.1 = ((bf16[4,80,640]{2,1,0:T(8,128)(2,1)}), bf16[4,80,640]{2,1,0:T(8,128)(2,1)S(1)}, u32[]{:S(2)}, u32[]{:S(2)}) async-start(bf16[4,80,640]{2,1,0:T(8,128)(2,1)} %bitcast.207), calls=%async_computation.1 | async-start | bytes 819200 | tf_op jit(solution)/shard_map/all_to_all | solution.py:366
  651.5 3.6 copy-start.39
  651.5 3.6 copy-start.40
  651.5 5.7 copy-start.25
  651.5 6.4 copy-start.23
  651.5 6.4 copy-start.24
  (19 other events, 40.2 us)
Sparse Core Ops, SparseCore 0:
  11.5 63.8 all-gather.3
  78.8 69.3 all-gather.5
  260.3 121.1 reduce-scatter.6
  383.7 156.8 reduce-scatter.8
  556.0 32.0 all-gather.7

commit v2 on v1

--- a/solution.py
+++ b/solution.py
@@ -136,9 +136,42 @@
 
 def attention_backward_kernel(
     qr_ref, kr_ref, vr_ref, do_ref, attn_ref, lse_ref, cos_ref, sin_ref, segc_ref, segr_ref,
-    dq_ref, dk_ref, dv_ref,
-    qt_s, dot_s, kt_s, delta_s, dqt_s, dk_s, dv_s,
+    *rest_refs,
 ):
+    if len(rest_refs) > 10:
+        parts_ref, dq_ref, dk_ref, dv_ref, own_ref = rest_refs[:5]
+        scratch = rest_refs[5:]
+        lanes = parts_ref.shape[-1] // 2
+        halves = [stages_of(parts_ref, scratch[7 + SUM_SCRATCH * n : 7 + SUM_SCRATCH * (n + 1)], pl.ds(n * lanes, lanes))
+                  for n in range(2)]
+    else:
+        halves = None
+        dq_ref, dk_ref, dv_ref = rest_refs[:3]
+        scratch = rest_refs[3:]
+    qt_s, dot_s, kt_s, delta_s, dqt_s, dk_s, dv_s = scratch[:7]
+    group = pl.program_id(0)
+    if halves is not None:
+        @pl.when(group == 0)
+        def _():
+            greet(all_partners())
+            halves[0].core_start()
+            halves[1].core_start()
+
+        @pl.when(group == 1)
+        def _():
+            halves[0].core_finish()
+            halves[0].chip_start()
+            halves[1].core_finish()
+
+        @pl.when(group == 2)
+        def _():
+            halves[1].chip_start()
+
+        @pl.when(group == 4)
+        def _():
+            halves[0].chip_finish()
+            halves[0].plane_start()
+
     tokens = qr_ref.shape[0]
     rest = tokens - LONGEST
     qt_s[...] = qr_ref[...].T
@@ -191,21 +224,39 @@
     dq_ref[...] = (pull(dqt_s[...].T) * (1.0 / math.sqrt(HEAD_DIM))).astype(jnp.bfloat16)
     dk_ref[...] = pull(dk_s[...]).astype(jnp.bfloat16)
     dv_ref[...] = dv_s[...].astype(jnp.bfloat16)
-
-
-def attention_backward(qr, kr, vr, attn_grad, attn, lse, cosine, sine, seg_col, seg_row):
+    if halves is not None:
+        @pl.when(group == 4)
+        def _():
+            halves[1].chip_finish()
+            halves[1].plane_start()
+            own_ref[:, :lanes] = halves[0].plane_finish()
+            own_ref[:, lanes:] = halves[1].plane_finish()
+
+
+def attention_backward(qr, kr, vr, attn_grad, attn, lse, cosine, sine, seg_col, seg_row, parts=None):
     tokens, width = qr.shape
     groups = width // LANES
     col = pl.BlockSpec((tokens, LANES), lambda g: (0, g))
     whole = lambda shape: pl.BlockSpec(shape, lambda g: (0,) * len(shape))
     flops = 10 * (LONGEST**2 + (tokens - LONGEST) ** 2) * 128 * groups * 4
+    with_sum = parts is not None
+    more_in, more_out, more_shape, more_scratch, more_params, more_args = [], [], [], [], {}, ()
+    if with_sum:
+        rows, lanes = parts.shape[-2:]
+        more_in = [pl.BlockSpec(memory_space=pl.ANY)]
+        more_out = [pl.BlockSpec((rows, lanes), lambda g: (0, 0))]
+        more_shape = [jax.ShapeDtypeStruct((rows, lanes), jnp.float32)]
+        more_scratch = sum_scratch(rows, lanes // 2) * 2
+        more_params = dict(collective_id=0, has_side_effects=True)
+        more_args = (parts,)
     return pl.pallas_call(
         attention_backward_kernel,
         grid=(groups,),
         in_specs=[col] * 5 + [pl.BlockSpec((1, 4, tokens), lambda g: (g, 0, 0)),
-                              whole((tokens, LANES)), whole((tokens, LANES)), whole((tokens, 1)), whole((1, tokens))],
-        out_specs=[col] * 3,
-        out_shape=[jax.ShapeDtypeStruct((tokens, width), jnp.bfloat16)] * 3,
+                              whole((tokens, LANES)), whole((tokens, LANES)), whole((tokens, 1)), whole((1, tokens))]
+        + more_in,
+        out_specs=[col] * 3 + more_out,
+        out_shape=[jax.ShapeDtypeStruct((tokens, width), jnp.bfloat16)] * 3 + more_shape,
         scratch_shapes=[
             pltpu.VMEM((LANES, tokens), jnp.bfloat16),
             pltpu.VMEM((LANES, tokens), jnp.bfloat16),
@@ -214,11 +265,202 @@
             pltpu.VMEM((LANES, tokens), jnp.float32),
             pltpu.VMEM((tokens, LANES), jnp.float32),
             pltpu.VMEM((tokens, LANES), jnp.float32),
-        ],
-        compiler_params=pltpu.CompilerParams(vmem_limit_bytes=48 << 20),
+        ] + more_scratch,
+        compiler_params=pltpu.CompilerParams(vmem_limit_bytes=56 << 20, **more_params),
         cost_estimate=pl.CostEstimate(flops=flops, bytes_accessed=20 << 20, transcendentals=20 << 20),
         name="attention_backward",
-    )(qr, kr, vr, attn_grad, attn, lse, cosine, sine, seg_col, seg_row)
+    )(qr, kr, vr, attn_grad, attn, lse, cosine, sine, seg_col, seg_row, *more_args)
+
+
+MESH = pl.DeviceIdType.MESH
+
+
+def place():
+    rank, plane = lax.axis_index("dp"), lax.axis_index("fsdp")
+    core = rank % 2
+    chip_x = (rank // 2) % 2
+    chip_y = rank // 4
+    return rank, plane, core, chip_x, chip_y
+
+
+def chip_at(step, chip_x, chip_y):
+    other_x = 1 - chip_x if step & 1 else chip_x
+    other_y = 1 - chip_y if step & 2 else chip_y
+    return 2 * other_y + other_x
+
+
+def greet(partners):
+    barrier = pltpu.get_barrier_semaphore()
+    for partner in partners:
+        pl.semaphore_signal(barrier, inc=1, device_id=partner, device_id_type=MESH)
+    pl.semaphore_wait(barrier, len(partners))
+
+
+def all_partners():
+    rank, plane, core, chip_x, chip_y = place()
+    sibling = 2 * chip_at(0, chip_x, chip_y) + 1 - core
+    partners = [(sibling, plane)]
+    partners += [(2 * chip_at(step, chip_x, chip_y) + core, plane) for step in (1, 2, 3)]
+    partners += [(rank, (plane + step) % 4) for step in (1, 2, 3)]
+    return partners
+
+
+class SumStages:
+    def __init__(self, parts, own, from_core, from_chip, from_plane, total, sems, lanes):
+        self.parts, self.own, self.from_core, self.from_chip = parts, own, from_core, from_chip
+        self.from_plane, self.total, self.lanes = from_plane, total, lanes
+        self.send, self.recv, self.local = sems
+        self.rank, self.plane, self.core, self.chip_x, self.chip_y = place()
+        self.chip = chip_at(0, self.chip_x, self.chip_y)
+
+    def remote(self, source, target, slot, device):
+        return pltpu.make_async_remote_copy(
+            src_ref=source, dst_ref=target, send_sem=self.send.at[slot], recv_sem=self.recv.at[slot],
+            device_id=device, device_id_type=MESH)
+
+    def core_copies(self):
+        load = pltpu.make_async_copy(self.parts.at[:, :, self.core, :, self.lanes], self.own, self.local)
+        give = self.remote(self.parts.at[:, :, 1 - self.core, :, self.lanes], self.from_core, 0,
+                           (2 * self.chip + 1 - self.core, self.plane))
+        return load, give
+
+    def core_start(self):
+        load, give = self.core_copies()
+        give.start()
+        load.start()
+
+    def core_finish(self):
+        load, give = self.core_copies()
+        load.wait()
+        give.wait()
+        for j in range(self.own.shape[0]):
+            self.own[j] = (self.own[j].astype(jnp.float32) + self.from_core[j].astype(jnp.float32)).astype(self.own.dtype)
+
+    def chip_copies(self):
+        return [
+            self.remote(self.own.at[:, chip_at(step, self.chip_x, self.chip_y)], self.from_chip.at[step - 1], step,
+                        (2 * chip_at(step, self.chip_x, self.chip_y) + self.core, self.plane))
+            for step in (1, 2, 3)
+        ]
+
+    def chip_start(self):
+        for copy in self.chip_copies():
+            copy.start()
+
+    def chip_finish(self):
+        for copy in self.chip_copies():
+            copy.wait()
+        for j in range(self.own.shape[0]):
+            value = self.own[j, pl.ds(self.chip, 1)][0].astype(jnp.float32)
+            for slot in range(3):
+                value = value + self.from_chip[slot, j].astype(jnp.float32)
+            self.total[j] = value.astype(self.total.dtype)
+
+    def plane_copies(self):
+        return [
+            self.remote(self.total.at[(self.plane + step) % 4], self.from_plane.at[step - 1], 3 + step,
+                        (self.rank, (self.plane + step) % 4))
+            for step in (1, 2, 3)
+        ]
+
+    def plane_start(self):
+        for copy in self.plane_copies():
+            copy.start()
+
+    def plane_finish(self):
+        for copy in self.plane_copies():
+            copy.wait()
+        value = self.total[pl.ds(self.plane, 1)][0].astype(jnp.float32)
+        for slot in range(3):
+            value = value + self.from_plane[slot].astype(jnp.float32)
+        return value
+
+
+def sum_scratch(rows, lanes, dtype=jnp.bfloat16):
+    return [
+        pltpu.VMEM((4, 4, rows, lanes), dtype),
+        pltpu.VMEM((4, 4, rows, lanes), dtype),
+        pltpu.VMEM((3, 4, rows, lanes), dtype),
+        pltpu.VMEM((3, rows, lanes), dtype),
+        pltpu.VMEM((4, rows, lanes), dtype),
+        pltpu.SemaphoreType.DMA((7,)),
+        pltpu.SemaphoreType.DMA((7,)),
+        pltpu.SemaphoreType.DMA,
+    ]
+
+
+SUM_SCRATCH = 8
+
+
+def stages_of(parts, scratch, lanes):
+    own, from_core, from_chip, from_plane, total, send, recv, local = scratch
+    return SumStages(parts, own, from_core, from_chip, from_plane, total, (send, recv, local), lanes)
+
+
+def table_sum(table_ref, table_out, from_core, from_chip, from_plane, held, send, recv):
+    rank, plane, core, chip_x, chip_y = place()
+    chip = chip_at(0, chip_x, chip_y)
+
+    def remote(source, target, slot, device):
+        return pltpu.make_async_remote_copy(
+            src_ref=source, dst_ref=target, send_sem=send.at[slot], recv_sem=recv.at[slot],
+            device_id=device, device_id_type=MESH)
+
+    give = remote(table_ref.at[:, 1 - core], from_core, 0, (2 * chip + 1 - core, plane))
+    give.start()
+    yield
+    give.wait()
+    held[...] = table_ref[:, pl.ds(core, 1)][:, 0] + from_core[...]
+    across = [remote(held.at[chip_at(step, chip_x, chip_y)], from_chip.at[step - 1], step,
+                     (2 * chip_at(step, chip_x, chip_y) + core, plane)) for step in (1, 2, 3)]
+    for copy in across:
+        copy.start()
+    yield
+    for copy in across:
+        copy.wait()
+    own = held[pl.ds(chip, 1)][0] + from_chip[0] + from_chip[1] + from_chip[2]
+    table_out[...] = own
+    along = [remote(table_out, from_plane.at[step - 1], 3 + step, (rank, (plane + step) % 4)) for step in (1, 2, 3)]
+    for copy in along:
+        copy.start()
+    yield
+    for copy in along:
+        copy.wait()
+    table_out[...] = own + from_plane[0] + from_plane[1] + from_plane[2]
+    yield
+
+
+def sum_kernel(parts_ref, table_ref, own_ref, table_out, *scratch):
+    stages = stages_of(parts_ref, scratch[:SUM_SCRATCH], pl.ds(0, parts_ref.shape[-1]))
+    small = table_sum(table_ref, table_out, *scratch[SUM_SCRATCH:])
+    greet(all_partners())
+    stages.core_start()
+    next(small)
+    stages.core_finish()
+    stages.chip_start()
+    next(small)
+    stages.chip_finish()
+    stages.plane_start()
+    next(small)
+    own_ref[...] = stages.plane_finish()
+    next(small)
+
+
+def sum_parts(parts, table):
+    rows, lanes = parts.shape[-2:]
+    vmem = pl.BlockSpec(memory_space=pltpu.VMEM)
+    tile = table.shape[-2:]
+    return pl.pallas_call(
+        sum_kernel,
+        in_specs=[pl.BlockSpec(memory_space=pl.ANY), vmem],
+        out_specs=[vmem, vmem],
+        out_shape=[jax.ShapeDtypeStruct((rows, lanes), jnp.float32), jax.ShapeDtypeStruct(tile, jnp.float32)],
+        scratch_shapes=sum_scratch(rows, lanes)
+        + [pltpu.VMEM((4, *tile), jnp.float32), pltpu.VMEM((3, *tile), jnp.float32), pltpu.VMEM((3, *tile), jnp.float32),
+           pltpu.VMEM((4, *tile), jnp.float32), pltpu.SemaphoreType.DMA((7,)), pltpu.SemaphoreType.DMA((7,))],
+        compiler_params=pltpu.CompilerParams(collective_id=1, has_side_effects=True, vmem_limit_bytes=40 << 20),
+        name="sum_parts",
+    )(parts, table)
 
 
 def row_layout(lengths, counts, row_len):
@@ -314,7 +556,19 @@
     branch_low = after_grad.astype(jnp.bfloat16)
     grad_t_out = tn(attn, branch_low)
     attn_grad = nt(branch_low, wt_out).astype(jnp.bfloat16)
-    dq, dk, dv = attention_backward(qr, kr, vr, attn_grad, attn, lse, cosine, sine, seg_col, seg_row)
+    near = (ranks, planes) == (8, 4)
+
+    def cut(values, j, rows):
+        return values[:, j * rows : (j + 1) * rows]
+
+    parts_b = jnp.stack([jnp.concatenate([cut(grad_t_up, j, r2), cut(grad_t_down, j, r3)], axis=1) for j in range(planes)])
+    if near:
+        parts_b = parts_b.astype(jnp.bfloat16).reshape(planes, 4, 2, columns, -1)
+        dq, dk, dv, own_b = attention_backward(
+            qr, kr, vr, attn_grad, attn, lse, cosine, sine, seg_col, seg_row, parts_b)
+    else:
+        dq, dk, dv = attention_backward(qr, kr, vr, attn_grad, attn, lse, cosine, sine, seg_col, seg_row)
+        own_b = lax.psum_scatter(parts_b.reshape(planes * width, -1), both, scatter_dimension=0, tiled=True)
     proj_grad = jnp.concatenate([dq, dk, dv], axis=1)
     grad_t_qkv = tn(normed_one, proj_grad)
     in_grad, gain_one, shift_one = pull_one(nt(proj_grad, wt_qkv))
@@ -333,15 +587,18 @@
     layer_out = turn_rows(layer_out, back)
     input_grad = turn_rows(input_grad, back)
 
-    def cut(values, j, rows):
-        return values[:, j * rows : (j + 1) * rows]
-
-    parts_b = jnp.stack([jnp.concatenate([cut(grad_t_up, j, r2), cut(grad_t_down, j, r3)], axis=1) for j in range(planes)])
-    own_b = lax.psum_scatter(parts_b.reshape(planes * width, -1), both, scatter_dimension=0, tiled=True)
-    parts_a = jnp.stack([jnp.concatenate([cut(grad_t_qkv, j, r0), cut(grad_t_out, j, r1), vector_grad.T], axis=1) for j in range(planes)])
-    own_a = lax.psum_scatter(parts_a.reshape(planes * width, -1), both, scatter_dimension=0, tiled=True)
+    if near:
+        parts_a = jnp.stack([jnp.concatenate([cut(grad_t_qkv, j, r0), cut(grad_t_out, j, r1)], axis=1) for j in range(planes)])
+        tiles = jnp.pad(vector_grad.reshape(n_vec, ranks, columns).transpose(1, 0, 2),
+                        ((0, 0), (0, 16 - n_vec), (0, LANES - columns))).reshape(4, 2, 16, LANES)
+        own_a, tile = sum_parts(parts_a.astype(jnp.bfloat16).reshape(planes, 4, 2, columns, -1), tiles)
+        vector_grad = tile[:n_vec, :columns]
+    else:
+        parts_a = jnp.stack([jnp.concatenate([cut(grad_t_qkv, j, r0), cut(grad_t_out, j, r1), vector_grad.T], axis=1)
+                             for j in range(planes)])
+        own_a = lax.psum_scatter(parts_a.reshape(planes * width, -1), both, scatter_dimension=0, tiled=True)
+        vector_grad = own_a[:, r0 + r1 :].T
     grads_t = (own_a[:, :r0], own_a[:, r0 : r0 + r1], own_b[:, :r2], own_b[:, r2:])
-    vector_grad = own_a[:, r0 + r1 :].T
     new_moments_t = [moment_keep * old.T + grad for old, grad in zip(old_moments, grads_t)]
 
     most = max(counts_rows)

time: 672 us -> 465 us (0.69)
  waiting for transfers between devices: 323 us -> 65.9 us
  Pallas kernels: 89.5 us -> 146 us
  other arithmetic: 55.6 us -> 47.6 us
    reduce_scatter x2 -> x0, waiting for transfers between devices: 254 us -> none  [the longest x1 155 us: shards(): lax.psum_scatter(parts_b.reshape(planes * width, -1), both, scatter_dimen...]
    pallas_call x0 -> x1, Pallas kernels: none -> 38.3 us  [sum_parts(): pl.pallas_call(sum_kernel, in_specs=[pl.BlockSpec(memory_space=pl.ANY), v...]
    pallas_call x1, Pallas kernels: 42.4 us -> 60.7 us  [attention_backward(): pl.pallas_call(attention_backward_kernel, grid=(groups,), in_specs=[col]...]
  transfers between devices with their start and end apart: 6 -> 4, of which waited for: 5 -> 3; matrix products, arithmetic and copies ran while one was open for 12% -> 14% of each run, Pallas kernels for 7% -> 10%
where the time goes in v2:
time: 465 us; the launch traced here: 459 us
  Pallas kernels  146 us (31%)
  matrix products  124 us (27%)
  waiting for transfers between devices  65.9 us (14%)
  other arithmetic  47.6 us (10%)
  local copies, waits for them, and re-layouts  37.1 us (8%)
  between operations  19.1 us (4%)
  blocking collectives  14.7 us (3%)
  starting transfers between devices  4.9 us (1%)
    pallas_call x1, Pallas kernels, attention_backward(): pl.pallas_call(attention_backward_kernel, grid=(groups,), in_specs=[col]...  60.7 us
    pallas_call x1, Pallas kernels, attention_forward(): pl.pallas_call(attention_forward_kernel, grid=(groups,), in_specs=[col(0)...  47.1 us
    all_gather x1, waiting for transfers between devices, shards(): lax.all_gather(slab_a, both, axis=0, tiled=True).reshape(planes, width, -1)  46.2 us
    dot_general x18, matrix products, high(): jnp.dot(left, right, precision=lax.Precision.HIGH, preferred_element_type...  44.9 us
    pallas_call x1, Pallas kernels, sum_parts(): pl.pallas_call(sum_kernel, in_specs=[pl.BlockSpec(memory_space=pl.ANY), v...  38.3 us
    dot_general x4, matrix products, nn(): return jnp.dot(left, right, preferred_element_type=jnp.float32)  34.3 us
    dot_general x5, matrix products, nt(): lax.dot_general(left, right, (((1,), (1,)), ((), ())), preferred_element_...  30.2 us
    all_gather x1, waiting for transfers between devices, shards(): whole = lax.all_gather(mine, 'dp', axis=0, tiled=True)  19.6 us
  transfers between devices with their start and end apart: 4, of which 3 were waited for; matrix products, arithmetic and copies ran while one was open for 14% of the time, Pallas kernels for 10%

profile of v2, /device:TPU:0, one launch (start us, length us, event | category | flops | bytes accessed | tf_op | source)
XLA Modules:
  0.0 459.2 jit_solution(3839728189005630613)
XLA Ops:
  29.3 46.2 %all-gather.4.cloned.1.call-done = bf16[2560,653]{1,0:T(8,128)(2,1)} async-done(((bf16[80,653]{1,0:T(8,128)(2,1)}), bf16[2560,653]{1,0:T(8,128)(2,1)}) %all-gather.4.cloned.1.call-update) | async-done | bytes 3343376 | tf_op jit(solution)/shard_map/all_gather | solution.py:523
  76.5 2.9 slice_bitcast_fusion.8
  79.5 5.2 %concatenate.93 = bf16[640,1920]{1,0:T(8,128)(2,1)} concatenate(bf16[640,480]{1,0:T(8,128)(2,1)} %get-tuple-element.113, bf16[640,480]{1,0:T(8,128)(2,1)} %get-tuple-element.112, bf16[640,480]{1,0:T(8,128)(2,1)S(1)} %get-tuple-element.111, bf16[640,480]{1,0:T(8,128)(2,1)S(1)} %get-tuple-element.110), dimensions={1} | concatenate | bytes 4915200 | tf_op jit(solution)/shard_map/concatenate | solution.py:526
  87.5 7.8 %broadcast_add_fusion.q_ref.k_ref.v_ref = f32[1024,1920]{1,0:T(8,128)} fusion(f32[1920]{0:T(1024)S(1)} %add.222, bf16[640,1920]{1,0:T(8,128)(2,1)} %concatenate.93, bf16[1024,640]{1,0:T(8,128)(2,1)S(1)} %copy-done.9, f32[640]{0:T(1024)S(1)} %get-tuple-element.85, f32[640]{0:T(1024)S(1)} %get-tuple-element.86, f32[1024]{0:T(1024)S(1)} %fusion.50, ...), kind=kOutput, calls=%fused_computation.12 | convolution fusion | flops 2522480640 | bytes 11653632 | tf_op jit(solution)/shard_map/dot_general | solution.py:42
  95.3 47.1 %attention_forward.1 = (bf16[1024,640]{1,0:T(8,128)(2,1)S(1)}, bf16[1024,640]{1,0:T(8,128)(2,1)S(1)}, bf16[1024,640]{1,0:T(8,128)(2,1)S(1)}, bf16[1024,640]{1,0:T(8,128)(2,1)}, f32[5,4,1024]{2,1,0:T(4,128)S(1)}) custom-call(f32[1024,1920]{1,0:T(8,128)} %broadcast_add_fusion.q_ref.k_ref.v_ref, f32[1024,1920]{1,0:T(8,128)} %broadcast_add_fusion.q_ref.k_ref.v_ref, ...), custom_call_target="tpu_custom_call" | custom-call | flops 6710886400 | bytes 20971520 | tf_op jit(solution)/shard_map/attention_forward/pallas_call | solution.py:118
  142.4 3.9 fusion.82
  148.4 3.6 slice_bitcast_fusion.3
  152.1 9.6 %multiply_convert_fusion = (bf16[1024,2560]{1,0:T(8,128)(2,1)}, f32[1024,2560]{1,0:T(8,128)}) fusion(f32[2560]{0:T(1024)S(1)} %add.238, bf16[640,640]{1,0:T(8,128)(2,1)S(1)} %get-tuple-element.102, bf16[640,640]{1,0:T(8,128)(2,1)S(1)} %get-tuple-element.103, bf16[640,640]{1,0:T(8,128)(2,1)S(1)} %get-tuple-element.104, ...), kind=kOutput, calls=%fused_computation.2 | convolution fusion | flops 3387555840 | bytes 21650432 | tf_op jit(solution)/shard_map/dot_general | solution.py:42
  161.7 13.0 %convert_reduce_fusion = (f32[2560]{0:T(1024)}, bf16[1024,2560]{1,0:T(8,128)(2,1)S(1)}) fusion(bf16[640,640]{1,0:T(8,128)(2,1)S(1)} %get-tuple-element.99, bf16[640,640]{1,0:T(8,128)(2,1)S(1)} %get-tuple-element.100, bf16[640,640]{1,0:T(8,128)(2,1)S(1)} %get-tuple-element.101, bf16[640,640]{1,0:T(8,128)(2,1)S(1)} %get-tuple-element.98, ...), kind=kOutput, calls=%fused_computation | convolution fusion | flops 3412456960 | bytes 20340736 | tf_op jit(solution)/shard_map/dot_general | solution.py:42
  174.7 5.2 %multiply_reduce_fusion = (f32[640]{0:T(1024)}, f32[1024]{0:T(1024)S(1)}, f32[640]{0:T(1024)}, f32[1024,640]{1,0:T(8,128)S(1)}) fusion(f32[1024,640]{1,0:T(8,128)S(1)} %copy-done.13, f32[1024]{0:T(1024)S(1)} %fusion.51, f32[1024]{0:T(1024)S(1)} %broadcast_multiply_fusion, f32[640]{0:T(1024)S(1)} %get-tuple-element.83, ...), kind=kOutput, calls=%fused_computation.46 | convolution fusion | flops 3373791232 | bytes 13782528 | tf_op jit(solution)/shard_map/dot_general | solution.py:46
  179.9 4.4 convolution_convert_fusion.1
  187.0 2.5 convolution_convert_fusion.4.do_ref
  190.8 4.1 convolution_convert_fusion
  196.0 3.4 pad_maximum_fusion.rest_refs_0_
  199.4 60.7 %attention_backward.1 = (bf16[1024,640]{1,0:T(8,128)(2,1)}, bf16[1024,640]{1,0:T(8,128)(2,1)}, bf16[1024,640]{1,0:T(8,128)(2,1)}, f32[80,1280]{1,0:T(8,128)}) custom-call(bf16[1024,640]{1,0:T(8,128)(2,1)} %copy-done.4, bf16[1024,640]{1,0:T(8,128)(2,1)} %copy-done.5, bf16[1024,640]{1,0:T(8,128)(2,1)} %copy-done.6, ...), custom_call_target="tpu_custom_call" | custom-call | flops 16777216000 | bytes 20971520 | tf_op jit(solution)/shard_map/attention_backward/pallas_call | solution.py:252
  264.5 5.6 %fusion.72 = (f32[640]{0:T(1024)}, f32[1024]{0:T(1024)}, f32[1024,640]{1,0:T(8,128)}) fusion(f32[640]{0:T(1024)S(1)} %get-tuple-element.86, f32[1024]{0:T(1024)S(1)} %broadcast_multiply_fusion.1, bf16[1024,640]{1,0:T(8,128)(2,1)S(1)} %copy-done.10, bf16[1024,1920]{1,0:T(8,128)(2,1)S(1)} %constant_dynamic-update-slice_fusion, ...), kind=kOutput, calls=%fused_computation.206 | convolution fusion | flops 2520513024 | bytes 10335232 | tf_op jit(solution)/shard_map/dot_general | solution.py:46
  270.1 4.7 %convolution_convert_fusion.3 = bf16[640,1920]{1,0:T(8,128)(2,1)} fusion(bf16[1024,1920]{1,0:T(8,128)(2,1)S(1)} %constant_dynamic-update-slice_fusion, bf16[1024,640]{1,0:T(8,128)(2,1)S(1)} %copy-done.10, f32[640]{0:T(1024)S(1)} %copy-done.61, f32[640]{0:T(1024)S(1)} %get-tuple-element.86, f32[1024]{0:T(1024)S(1)} %fusion.50, ...), kind=kOutput, calls=%fused_computation.29 | convolution fusion | flops 2521743360 | bytes 7713792 | tf_op jit(solution)/shard_map/dot_general | solution.py:50
  282.1 3.5 fusion.8
  285.8 2.9 fusion.80
  290.7 38.3 %sum_parts.1 = (f32[80,640]{1,0:T(8,128)S(1)}, f32[16,128]{1,0:T(8,128)S(1)}) custom-call(bf16[4,4,2,80,640]{4,3,2,1,0:T(8,128)(2,1)S(1)} %pad_maximum_fusion.3.parts_ref, f32[4,2,16,128]{3,2,1,0:T(8,128)S(1)} %bitcast.190), custom_call_target="tpu_custom_call" | custom-call | tf_op jit(solution)/shard_map/sum_parts/pallas_call | solution.py:453
  331.4 14.7 %all_to_all.10 = bf16[4,80,640]{2,1,0:T(8,128)(2,1)S(1)} all-to-all(bf16[4,80,640]{2,1,0:T(8,128)(2,1)S(1)} %pad_maximum_fusion.17), channel_id=1, replica_groups=mesh['dp'=8,'fsdp'=4] {'fsdp'}, dimensions={0} | all-to-all | bytes 819200 | tf_op jit(solution)/shard_map/all_to_all | solution.py:607
  348.9 9.6 %add_convert_fusion.1 = bf16[1024,640]{1,0:T(8,128)(2,1)} fusion(f32[1024,640]{1,0:T(8,128)} %copy-done.12, bf16[1024,2560]{1,0:T(8,128)(2,1)} %get-tuple-element.146, f32[640]{0:T(1024)S(1)} %copy-done.59, bf16[640,640]{1,0:T(8,128)(2,1)} %copy-done.26, bf16[640,640]{1,0:T(8,128)(2,1)} %copy-done.27, bf16[640,640]{1,0:T(8,128)(2,1)} %copy-done.28, ...), kind=kOutput, calls=%fused_computation.52 | convolution fusion | flops 3370516480 | bytes 12454400 | tf_op jit(solution)/shard_map/dot_general | solution.py:46
  358.5 19.6 %all-gather.8.cloned.1.call-done = bf16[640,2560]{1,0:T(8,128)(2,1)} async-done(((bf16[80,2560]{1,0:T(8,128)(2,1)}), bf16[640,2560]{1,0:T(8,128)(2,1)}) %all-gather.8.cloned.1.call-update) | async-done | bytes 3276816 | tf_op jit(solution)/shard_map/all_gather | solution.py:609
  378.0 7.4 %select_reduce_fusion = (f32[]{:T(128)}, f32[640,640]{1,0:T(8,128)}) fusion(bf16[640,2560]{1,0:T(8,128)(2,1)} %all-gather.8.cloned.1.call-done), kind=kOutput, calls=%fused_computation.67 | convolution fusion | flops 2098380800 | bytes 4915204 | tf_op jit(solution)/shard_map/dot_general | solution.py:46
  386.1 5.2 %fusion.13 = f32[640,640]{1,0:T(8,128)S(1)} fusion(f32[640,640]{1,0:T(8,128)} %get-tuple-element.153, f32[]{:T(128)S(6)} %add.254), kind=kOutput, calls=%fused_computation.55 | convolution fusion | flops 1576140800 | bytes 3276804 | tf_op jit(solution)/shard_map/dot_general | solution.py:502
  396.1 2.5 fusion.14
  408.0 2.6 fusion.88
  420.0 2.8 fusion.92
  432.1 4.8 %all-to-all-start.1 = ((bf16[4,80,640]{2,1,0:T(8,128)(2,1)}), bf16[4,80,640]{2,1,0:T(8,128)(2,1)S(1)}, u32[]{:S(2)}, u32[]{:S(2)}) async-start(bf16[4,80,640]{2,1,0:T(8,128)(2,1)} %bitcast.189), calls=%async_computation.1 | async-start | bytes 819200 | tf_op jit(solution)/shard_map/all_to_all | solution.py:623
  436.9 4.3 add_add_fusion.2
  441.9 3.8 fusion.24
  445.7 2.8 fusion.11
  (257 shorter events, 85.7 us)
Async XLA Ops:
  7.2 13.5 %copy-start.64 = (s32[1,4]{1,0:T(1,128)S(1)}, s32[1,4]{1,0:T(1,128)}, u32[]{:S(2)}) copy-start(s32[1,4]{1,0:T(1,128)} %param.18) | copy-start | bytes 52
  7.2 13.6 %copy-start.23 = (bf16[1024,640]{1,0:T(8,128)(2,1)S(1)}, bf16[1024,640]{1,0:T(8,128)(2,1)}, u32[]{:S(2)}) copy-start(bf16[1024,640]{1,0:T(8,128)(2,1)} %param.16) | copy-start | bytes 3932164
  7.2 68.2 %all-gather.4.cloned.1.call-start = ((), (), s32[]{:S(2)}) async-start(), calls=%async_computation.2 | async-start | bytes 4055040 | tf_op jit(solution)/shard_map/all_gather | solution.py:523
  10.9 137.5 %all-gather.6.cloned.1.call-start = ((), (), s32[]{:S(2)}) async-start(), calls=%async_computation.3 | async-start | bytes 6758400 | tf_op jit(solution)/shard_map/all_gather | solution.py:524
  12.7 365.3 %all-gather.8.cloned.1.call-start = ((), (), s32[]{:S(2)}) async-start(), calls=%async_computation.4 | async-start | bytes 3686400 | tf_op jit(solution)/shard_map/all_gather | solution.py:609
  19.8 75.5 %copy-start.3 = (s32[1024]{0:T(1024)}, s32[1024]{0:T(1024)S(1)}, u32[]{:S(2)}) copy-start(s32[1024]{0:T(1024)S(1)} %convert_reduce_fusion.5) | copy-start | bytes 12292
  20.0 75.3 %copy-start.2 = (s32[1024,1]{1,0:T(8,128)}, s32[1024,1]{1,0:T(8,128)S(1)}, u32[]{:S(2)}) copy-start(s32[1024,1]{1,0:T(8,128)S(1)} %copy.52.segc_ref) | copy-start | bytes 12292
  27.3 242.8 %copy-start.47 = (f32[1024]{0:T(1024)}, f32[1024]{0:T(1024)S(1)}, u32[]{:S(2)}) copy-start(f32[1024]{0:T(1024)S(1)} %fusion.50) | copy-start | bytes 12292
  29.2 66.1 %copy-start = (f32[1024,128]{1,0:T(8,128)}, f32[1024,128]{1,0:T(8,128)S(1)}, u32[]{:S(2)}) copy-start(f32[1024,128]{1,0:T(8,128)S(1)} %get-tuple-element.142.sin_ref) | copy-start | bytes 1572868
  29.2 66.1 %copy-start.1 = (f32[1024,128]{1,0:T(8,128)}, f32[1024,128]{1,0:T(8,128)S(1)}, u32[]{:S(2)}) copy-start(f32[1024,128]{1,0:T(8,128)S(1)} %get-tuple-element.143.cos_ref) | copy-start | bytes 1572868
  85.3 10.0 %copy-start.60 = (f32[640]{0:T(1024)}, f32[640]{0:T(1024)S(1)}, u32[]{:S(2)}) copy-start(f32[640]{0:T(1024)S(1)} %get-tuple-element.85) | copy-start | bytes 7684
  85.3 184.8 %copy-start.42 = (f32[640]{0:T(1024)}, f32[640]{0:T(1024)S(1)}, u32[]{:S(2)}) copy-start(f32[640]{0:T(1024)S(1)} %get-tuple-element.86) | copy-start | bytes 7684
  87.5 55.0 %copy-start.32 = (bf16[640,160]{1,0:T(8,128)(2,1)}, bf16[640,160]{1,0:T(8,128)(2,1)S(1)}, u32[]{:S(2)}) copy-start(bf16[640,160]{1,0:T(8,128)(2,1)S(1)} %get-tuple-element.108) | copy-start | bytes 614404
  87.5 55.0 %copy-start.34 = (bf16[640,160]{1,0:T(8,128)(2,1)}, bf16[640,160]{1,0:T(8,128)(2,1)S(1)}, u32[]{:S(2)}) copy-start(bf16[640,160]{1,0:T(8,128)(2,1)S(1)} %get-tuple-element.109) | copy-start | bytes 614404
  152.0 9.7 %copy-start.24 = (bf16[640,640]{1,0:T(8,128)(2,1)}, bf16[640,640]{1,0:T(8,128)(2,1)S(1)}, u32[]{:S(2)}) copy-start(bf16[640,640]{1,0:T(8,128)(2,1)S(1)} %get-tuple-element.98) | copy-start | bytes 2457604
  152.0 9.7 %copy-start.26 = (bf16[640,640]{1,0:T(8,128)(2,1)}, bf16[640,640]{1,0:T(8,128)(2,1)S(1)}, u32[]{:S(2)}) copy-start(bf16[640,640]{1,0:T(8,128)(2,1)S(1)} %get-tuple-element.99) | copy-start | bytes 2457604
  152.0 9.7 %copy-start.27 = (bf16[640,640]{1,0:T(8,128)(2,1)}, bf16[640,640]{1,0:T(8,128)(2,1)S(1)}, u32[]{:S(2)}) copy-start(bf16[640,640]{1,0:T(8,128)(2,1)S(1)} %get-tuple-element.100) | copy-start | bytes 2457604
  152.0 9.7 %copy-start.28 = (bf16[640,640]{1,0:T(8,128)(2,1)}, bf16[640,640]{1,0:T(8,128)(2,1)S(1)}, u32[]{:S(2)}) copy-start(bf16[640,640]{1,0:T(8,128)(2,1)S(1)} %get-tuple-element.101) | copy-start | bytes 2457604
  152.1 9.6 %copy-start.11 = (bf16[1024,640]{1,0:T(8,128)(2,1)S(1)}, bf16[1024,640]{1,0:T(8,128)(2,1)}, u32[]{:S(2)}) copy-start(bf16[1024,640]{1,0:T(8,128)(2,1)} %get-tuple-element.91) | copy-start | bytes 3932164
  274.8 7.3 %copy-start.43 = (f32[640]{0:T(1024)S(1)}, f32[640]{0:T(1024)}, u32[]{:S(2)}) copy-start(f32[640]{0:T(1024)} %copy-done.42) | copy-start | bytes 7684
  281.3 7.4 %copy-start.45 = (f32[1024]{0:T(1024)}, f32[1024]{0:T(1024)S(1)}, u32[]{:S(2)}) copy-start(f32[1024]{0:T(1024)S(1)} %multiply_multiply_fusion.1) | copy-start | bytes 12292
  290.6 39.1 %copy-start.41 = (f32[480,80]{0,1:T(8,128)S(1)}, f32[480,80]{0,1:T(8,128)}, u32[]{:S(2)}) copy-start(f32[480,80]{0,1:T(8,128)} %param.23) | copy-start | bytes 460804
  290.6 39.9 %copy-start.31 = (f32[80,1280]{1,0:T(8,128)S(1)}, f32[80,1280]{1,0:T(8,128)}, u32[]{:S(2)}) copy-start(f32[80,1280]{1,0:T(8,128)} %get-tuple-element.33) | copy-start | bytes 1228804
  290.6 39.9 %copy-start.39 = (f32[640,80]{0,1:T(8,128)S(1)}, f32[640,80]{0,1:T(8,128)}, u32[]{:S(2)}) copy-start(f32[640,80]{0,1:T(8,128)} %param.25) | copy-start | bytes 614404
  290.6 39.9 %copy-start.40 = (f32[640,80]{0,1:T(8,128)S(1)}, f32[640,80]{0,1:T(8,128)}, u32[]{:S(2)}) copy-start(f32[640,80]{0,1:T(8,128)} %param.26) | copy-start | bytes 614404
  329.7 18.4 %copy-start.36 = (f32[160,80]{1,0:T(8,128)S(1)}, f32[160,80]{1,0:T(8,128)}, u32[]{:S(2)}) copy-start(f32[160,80]{1,0:T(8,128)} %param.20) | copy-start | bytes 153604
  329.7 19.1 %copy-start.56 = (f32[1024]{0:T(1024)S(1)}, f32[1024]{0:T(1024)}, u32[]{:S(2)}) copy-start(f32[1024]{0:T(1024)} %get-tuple-element.77) | copy-start | bytes 12292
  329.7 19.1 %copy-start.25 = (bf16[640,640]{1,0:T(8,128)(2,1)S(1)}, bf16[640,640]{1,0:T(8,128)(2,1)}, u32[]{:S(2)}) copy-start(bf16[640,640]{1,0:T(8,128)(2,1)} %copy-done.24) | copy-start | bytes 2457604
  329.8 19.1 %copy-start.59 = (f32[640]{0:T(1024)S(1)}, f32[640]{0:T(1024)}, u32[]{:S(2)}) copy-start(f32[640]{0:T(1024)} %get-tuple-element.81) | copy-start | bytes 7684
  429.9 6.9 %copy-start.44 = (f32[640]{0:T(1024)S(1)}, f32[640]{0:T(1024)}, u32[]{:S(2)}) copy-start(f32[640]{0:T(1024)} %copy-done.42) | copy-start | bytes 7684
  429.9 6.9 %copy-start.46 = (f32[1024]{0:T(1024)S(1)}, f32[1024]{0:T(1024)}, u32[]{:S(2)}) copy-start(f32[1024]{0:T(1024)} %copy-done.45) | copy-start | bytes 12292
  432.1 17.2 %all-to-all-start.1 = ((bf16[4,80,640]{2,1,0:T(8,128)(2,1)}), bf16[4,80,640]{2,1,0:T(8,128)(2,1)S(1)}, u32[]{:S(2)}, u32[]{:S(2)}) async-start(bf16[4,80,640]{2,1,0:T(8,128)(2,1)} %bitcast.189), calls=%async_computation.1 | async-start | bytes 819200 | tf_op jit(solution)/shard_map/all_to_all | solution.py:623
  (41 other events, 147.5 us)
Sparse Core Ops, SparseCore 0:
  11.5 63.8 all-gather.3
  78.8 69.2 all-gather.5
  347.0 30.9 all-gather.7
